TPU v7x, 128 devices: a whole 4x4x4 slice. The times are simulated.
128 devices in a mesh: seq: 8 (over y_lo, z), chan: 16 (over x, y_hi, core).
Axes of the slice: x: 4, y: 4 (y_hi: 2, y_lo: 2; y = y_hi * 2 + y_lo), z: 4, core: 2. Of those that a mesh axis runs over, the one named last changes fastest.
Arguments:
- resid: bfloat16 [16384, 4096], P('seq', 'chan'), may hold values from -1100 to 1100
- norm_gain: bfloat16 [4096], P('chan'), may hold values from 0.5 to 1.5
- feat_weight: bfloat16 [4096, 3, 4096], P(None, None, 'chan'), may hold values from -0.09375 to 0.09375
- short_filter: float32 [3, 3, 4096], P(None, None, 'chan'), may hold values from -3.5 to 3.5
- mr_filter: bfloat16 [128, 4096], P(None, 'chan'), may hold values from -0.5 to 0.5
- gates_lr: bfloat16 [16384, 2, 4096], P('seq', None, 'chan'), may hold values from -6 to 6
- decay_rate: float32 [16, 4096], P(None, 'chan'), may hold values from 1.2207031e-06 to 0.0333333333
- residue: float32 [16, 4096], P(None, 'chan'), may hold values from -1.5 to 1.5
- skip_gain: float32 [4096], P('chan'), may hold values from 0.5 to 1.5
Outputs:
- mixed: bfloat16 [16384, 4096], P('seq', 'chan')
All inputs are finite; a program needn't handle non-finite values.
Results may differ from a plain program's by a relative error of at most 0.012.
Values may be sent and summed in bfloat16 or wider, within the bound.
A program may use at most 128 MiB of HBM per device.

v0:
```python
import jax
import jax.numpy as jnp
from jax import lax
from jax.sharding import PartitionSpec as P

D = 4096


tile_rows = 128
norm_epsilon = 1e-05
highest = lax.Precision.HIGHEST


def shifted(value, axis, by):
    peers = lax.axis_size(axis)
    pairs = [(i, i + by) for i in range(peers) if 0 <= i + by < peers]
    return lax.ppermute(value, axis, pairs)


def as_sent(value):

    def short(part):
        return part.astype(jnp.bfloat16) if part.dtype == jnp.float32 else part

    return jax.tree.map(short, value)


def combine_states(earlier, later):
    return (earlier[0] * later[0], later[0] * earlier[1] + later[1])


def featurize(padded, short_filter, count):
    short_len = short_filter.shape[0]
    total = jnp.zeros((count,) + padded.shape[1:], jnp.float32)
    for tap_index in range(short_len):
        start_row = short_len - 1 - tap_index
        total = (
            total
            + padded[start_row : start_row + count].astype(jnp.float32)
            * short_filter[tap_index][None]
        )
    return total


def depthwise(signal, taps, front, precision_kind, out_type):
    channels = signal.shape[2]
    kernel = taps[::-1][:, None, :]
    return lax.conv_general_dilated(
        signal,
        kernel,
        (1,),
        ((front, 0),),
        dimension_numbers=("NWC", "WIO", "NWC"),
        feature_group_count=channels,
        precision=precision_kind,
        preferred_element_type=out_type,
    )


def medium_conv(z_full, mr_filter, length):
    result = depthwise(z_full[None], mr_filter, 0, None, jnp.float32)
    return result[0, :length]


def modal_local(z_long, decays, residues):
    length, channels = z_long.shape
    blocks = length // tile_rows
    values = z_long.astype(jnp.float32).reshape(blocks, tile_rows, channels)
    offsets = jnp.arange(tile_rows, dtype=jnp.float32)
    weighted = residues * jnp.sqrt(-jnp.expm1(-2.0 * decays))
    powers = jnp.exp(-decays[None] * offsets[:, None, None])
    tap_values = jnp.sum(powers * weighted[None], axis=1)
    within = depthwise(values, tap_values, tile_rows - 1, highest, jnp.float32)
    end_powers = jnp.exp(-decays[None] * (tile_rows - 1.0 - offsets)[:, None, None])
    block_ends = jnp.sum(end_powers[None] * values[:, :, None, :], axis=1)
    step_decay = jnp.broadcast_to(jnp.exp(-decays * tile_rows)[None], block_ends.shape)
    _, inclusive = lax.associative_scan(combine_states, (step_decay, block_ends), axis=0)
    starts = jnp.concatenate([jnp.zeros_like(inclusive[:1]), inclusive[:-1]], axis=0)
    return (within, starts, inclusive[-1])


def modal_finish(within, starts, incoming, decays, residues):
    blocks, _, channels = within.shape
    offsets = jnp.arange(tile_rows, dtype=jnp.float32)
    weighted = residues * jnp.sqrt(-jnp.expm1(-2.0 * decays))
    block_index = jnp.arange(blocks, dtype=jnp.float32)
    starts = (
        starts + jnp.exp(-decays[None] * (tile_rows * block_index)[:, None, None]) * incoming[None]
    )
    out_powers = weighted[None] * jnp.exp(-decays[None] * (offsets + 1.0)[:, None, None])
    carried = jnp.sum(out_powers[None] * starts[:, None, :, :], axis=2)
    return (within + carried).reshape(blocks * tile_rows, channels)


def on_device(
    resid, norm_gain, feat_weight, short_filter, mr_filter, gates_lr, decay_rate, residue, skip_gain
):
    tokens, channels = resid.shape
    flat_weight = feat_weight.reshape(feat_weight.shape[0], 3 * channels)
    values = resid.astype(jnp.float32)
    squares = lax.psum(jnp.sum(values * values, axis=1), "chan")
    inv_scale = lax.rsqrt(squares / D + norm_epsilon)
    normed = (values * inv_scale[:, None] * norm_gain.astype(jnp.float32)[None]).astype(
        jnp.bfloat16
    )
    projected = jnp.dot(
        lax.all_gather(normed, "chan", axis=1, tiled=True),
        flat_weight,
        preferred_element_type=jnp.float32,
    )
    stream_rows = projected.astype(jnp.bfloat16).reshape(tokens, 3, channels)
    short_len = short_filter.shape[0]
    tap_count = mr_filter.shape[0]
    head_rows = shifted(stream_rows[tokens - (short_len - 1) :], "seq", 1)
    featured = featurize(jnp.concatenate([head_rows, stream_rows], axis=0), short_filter, tokens)
    product = (featured[:, 1] * featured[:, 2]).astype(jnp.bfloat16)
    rim_rows = shifted(product[tokens - (tap_count - 1) :], "seq", 1)
    query_gate = featured[:, 0]
    z_full = jnp.concatenate([rim_rows, product], axis=0)
    medium = medium_conv(z_full, mr_filter, tokens)
    mixed_mr = (query_gate * medium).astype(jnp.bfloat16)
    gates = gates_lr.astype(jnp.float32)
    long_input = (gates[:, 1] * mixed_mr.astype(jnp.float32)).astype(jnp.bfloat16)
    spread = lax.all_to_all(long_input, "seq", split_axis=1, concat_axis=0, tiled=True)
    narrow = spread.shape[1]
    first_channel = lax.axis_index("seq") * narrow
    decay_part = lax.dynamic_slice_in_dim(decay_rate, first_channel, narrow, 1)
    residue_part = lax.dynamic_slice_in_dim(residue, first_channel, narrow, 1)
    within, starts, _ = modal_local(spread, decay_part, residue_part)
    whole_conv = modal_finish(within, starts, jnp.zeros_like(decay_part), decay_part, residue_part)
    long_out = lax.all_to_all(
        as_sent(whole_conv), "seq", split_axis=0, concat_axis=1, tiled=True
    ).astype(whole_conv.dtype)
    return (gates[:, 0] * (long_out + skip_gain[None] * long_input.astype(jnp.float32))).astype(
        jnp.bfloat16
    )


def solution(mesh):
    in_specs = (
        P("seq", "chan"),
        P("chan"),
        P(None, None, "chan"),
        P(None, None, "chan"),
        P(None, "chan"),
        P("seq", None, "chan"),
        P(None, "chan"),
        P(None, "chan"),
        P("chan"),
    )
    out_specs = P("seq", "chan")
    return jax.shard_map(
        on_device, mesh=mesh, in_specs=in_specs, out_specs=out_specs, check_vma=False
    )
```

profile of v0, /device:TPU:0, one launch (start us, length us, event | category | flops | bytes accessed | tf_op | source)
XLA Modules:
  0.0 612.5 jit_solution(5045128516159069623)
XLA Ops:
  8.1 38.6 %psum.7 = f32[2048]{0:T(1024)S(1)} all-reduce(f32[2048]{0:T(1024)S(1)} %fusion.2), channel_id=1, replica_groups=mesh['seq'=8,'chan'=16] {'chan'}, use_global_device_ids=true, to_apply=%region_1.0 | all-reduce | flops 2048 | bytes 16384 | tf_op jit(solution)/shard_map/psum | solution.py:101
  49.9 8.8 %copy.172 = bf16[4096,3,256]{0,2,1:T(8,128)(2,1)} copy(bf16[4096,3,256]{2,0,1:T(8,128)(2,1)} %param.11) | data formatting | bytes 12582912 | tf_op args[2]
  58.7 112.0 %all-gather.2.cloned.1.call-done = bf16[2048,4096]{1,0:T(8,128)(2,1)} async-done(((bf16[2048,256]{1,0:T(8,128)(2,1)}), bf16[2048,4096]{1,0:T(8,128)(2,1)}) %all-gather.2.cloned.1.call-update) | async-done | bytes 16777232 | tf_op jit(solution)/shard_map/all_gather | solution.py:107
  170.7 18.2 %convolution_convert_fusion = bf16[2048,768]{1,0:T(8,128)(2,1)S(1)} fusion(bf16[2048,4096]{1,0:T(8,128)(2,1)} %all-gather.2.cloned.1.call-done, bf16[4096,768]{0,1:T(8,128)(2,1)} %bitcast.84), kind=kOutput, calls=%fused_computation.3 | convolution fusion | flops 12886474752 | bytes 26214400 | tf_op jit(solution)/shard_map/dot_general | solution.py:106
  194.2 4.7 copy.173
  199.0 8.2 %multiply_add_fusion = f32[2048,3,256]{0,2,1:T(8,128)S(1)} fusion(bf16[2048,3,256]{0,2,1:T(8,128)(2,1)} %bitcast.76, bf16[2,3,256]{0,2,1:T(8,128)(2,1)S(1)} %collective-permute-done, f32[3,256]{1,0:T(4,128)S(1)} %get-tuple-element.19, f32[3,256]{1,0:T(4,128)S(1)} %get-tuple-element.20, f32[3,256]{1,0:T(4,128)S(1)} %get-tuple-element.18), kind=kLoop, calls=%fused_computation.2 | loop fusion | flops 22020096 | bytes 9449472 | tf_op jit(solution)/shard_map/add | solution.py:38
  210.5 4.2 collective-permute-start.1
  214.8 4.7 copy.171
  225.5 47.9 %fusion.17 = f32[8,272,256]{2,0,1:T(8,128)S(1)} fusion(pred[8,272]{0,1:T(8,128)(4,1)S(1)} %copy-done.19, bf16[128,1,256]{2,0,1:T(8,128)(2,1)S(1)} %bitcast.90, bf16[8,399,256]{2,0,1:T(8,128)(2,1)S(1)} %fusion.44), kind=kOutput, calls=%fused_computation.34 | convolution fusion | flops 143163392 | bytes 3930240 | tf_op jit(solution)/shard_map/conv_general_dilated | solution.py:48
  278.5 4.3 multiply_convert_fusion
  282.8 5.1 all-to-all-start
  290.9 11.1 %all-to-all-done = bf16[2048,8,32]{0,2,1:T(8,128)(2,1)S(1)} async-done(((bf16[2048,8,32]{0,2,1:T(8,128)(2,1)}), bf16[2048,8,32]{0,2,1:T(8,128)(2,1)S(1)}, u32[]{:S(2)}, u32[]{:S(2)}) %all-to-all-start) | async-done | bytes 1048608 | tf_op jit(solution)/shard_map/all_to_all | solution.py:124
  305.8 9.3 %multiply_reduce_fusion.1 = f32[128,16,32]{2,1,0:T(8,128)S(1)} fusion(f32[128,128,32]{1,2,0:T(8,128)S(1)} %copy.184, f32[128,16,32]{0,2,1:T(8,128)S(1)} %get-tuple-element.21), kind=kLoop, calls=%fused_computation.1 | loop fusion | flops 16711680 | bytes 2621440 | tf_op jit(solution)/shard_map/reduce_sum | solution.py:75
  322.3 3.7 slice.212
  326.1 3.8 slice.213
  363.5 4.5 slice.246
  383.4 6.6 %pad.51 = f32[16,16,32]{0,2,1:T(8,128)S(1)} pad(f32[8,16,32]{0,2,1:T(8,128)} %add.145, f32[]{:T(128)} %constant.12.clone.1), padding=1_0_1x0_0_0x0_0_0 | pad | bytes 49156 | tf_op jit(solution)/shard_map/pad | solution.py:77
  401.1 7.6 %pad.55 = f32[64,16,32]{0,2,1:T(8,128)S(1)} pad(f32[32,16,32]{0,2,1:T(8,128)} %add.149, f32[]{:T(128)} %constant.12.clone.1), padding=1_0_1x0_0_0x0_0_0 | pad | bytes 196612 | tf_op jit(solution)/shard_map/pad | solution.py:77
  409.4 10.6 %pad.126 = f32[128,16,32]{0,2,1:T(8,128)} pad(f32[64,16,32]{0,2,1:T(8,128)} %add.151, f32[]{:T(128)} %constant.12.clone.1), padding=1_0_1x0_0_0x0_0_0 | pad | bytes 393220
  422.5 5.3 pad.82
  428.6 13.2 %multiply_reduce_fusion = f32[128,128,32]{1,2,0:T(8,128)} fusion(f32[128,16,32]{2,1,0:T(8,128)S(1)} %copy.191, f32[128,16,32]{0,2,1:T(8,128)} %get-tuple-element.16), kind=kLoop, calls=%fused_computation | loop fusion | flops 16252928 | bytes 2621440 | tf_op jit(solution)/shard_map/reduce_sum | solution.py:91
  445.3 129.8 %add_convert_fusion = bf16[128,128,32]{0,2,1:T(8,128)(2,1)} fusion(f32[128,128,32]{0,2,1:T(8,128)} %copy.192, bf16[128,128,32]{0,2,1:T(8,128)(2,1)S(1)} %copy-done.8, f32[128,1,32]{2,1,0:T(1,128)S(1)} %copy.183), kind=kOutput, calls=%fused_computation.25 | convolution fusion | flops 406847488 | bytes 4210688 | tf_op jit(solution)/shard_map/conv_general_dilated | solution.py:48
  587.4 12.4 %all-to-all-done.1 = bf16[8,2048,32]{1,2,0:T(8,128)(2,1)S(1)} async-done(((bf16[8,2048,32]{1,2,0:T(8,128)(2,1)}), bf16[8,2048,32]{1,2,0:T(8,128)(2,1)S(1)}, u32[]{:S(2)}, u32[]{:S(2)}) %all-to-all-start.1) | async-done | bytes 1048608 | tf_op jit(solution)/shard_map/all_to_all | solution.py:131
  599.8 4.5 fusion.7
  (140 shorter events, 119.3 us)
Async XLA Ops:
  6.5 164.2 %all-gather.2.cloned.1.call-start = ((), (), s32[]{:S(2)}) async-start(), calls=%async_computation.2 | async-start | bytes 17825792 | tf_op jit(solution)/shard_map/all_gather | solution.py:107
  170.7 23.5 %copy-start.15 = (f32[3,3,256]{2,1,0:T(4,128)S(1)}, f32[3,3,256]{2,1,0:T(4,128)}, u32[]{:S(2)}) copy-start(f32[3,3,256]{2,1,0:T(4,128)} %param.12) | copy-start | bytes 27652
  188.9 1.6 copy-start.9
  190.7 8.2 %collective-permute-start = (bf16[2,3,256]{0,2,1:T(8,128)(2,1)S(1)}, bf16[2,3,256]{0,2,1:T(8,128)(2,1)S(1)}, u32[]{:S(2)}, u32[]{:S(2)}) collective-permute-start(bf16[2,3,256]{0,2,1:T(8,128)(2,1)S(1)} %bitcast.88), channel_id=1, source_target_pairs={{0,16},{16,32},{32,48},{48,64},{64,80},{80,96},{96,112},{1,17},{17... | collective-permute-start | bytes 9224 | tf_op jit(solution)/shard_map/ppermute | solution.py:17
  207.2 3.3 copy-start
  207.2 7.6 %copy-start.14 = (bf16[128,256]{1,0:T(8,128)(2,1)S(1)}, bf16[128,256]{1,0:T(8,128)(2,1)}, u32[]{:S(2)}) copy-start(bf16[128,256]{1,0:T(8,128)(2,1)} %param.13) | copy-start | bytes 196612
  210.5 10.7 %collective-permute-start.1 = (bf16[127,256]{0,1:T(8,128)(2,1)S(1)}, bf16[127,256]{0,1:T(8,128)(2,1)S(1)}, u32[]{:S(2)}, u32[]{:S(2)}) collective-permute-start(bf16[127,256]{0,1:T(8,128)(2,1)S(1)} %slice_bitcast_fusion.1), channel_id=1, source_target_pairs={{0,16},{16,32},{32,48},{48,64},{64,80},{80,96},{96,112},{1,17},{17... | collective-permute-start | bytes 195080 | tf_op jit(solution)/shard_map/ppermute | solution.py:17
  278.5 9.4 %copy-start.16 = (f32[16,256]{1,0:T(8,128)S(1)}, f32[16,256]{1,0:T(8,128)}, u32[]{:S(2)}) copy-start(f32[16,256]{1,0:T(8,128)} %param.15) | copy-start | bytes 49156
  278.5 9.4 %copy-start.17 = (f32[16,256]{1,0:T(8,128)S(1)}, f32[16,256]{1,0:T(8,128)}, u32[]{:S(2)}) copy-start(f32[16,256]{1,0:T(8,128)} %param.16) | copy-start | bytes 49156
  282.8 19.2 %all-to-all-start = ((bf16[2048,8,32]{0,2,1:T(8,128)(2,1)}), bf16[2048,8,32]{0,2,1:T(8,128)(2,1)S(1)}, u32[]{:S(2)}, u32[]{:S(2)}) async-start(bf16[2048,8,32]{0,2,1:T(8,128)(2,1)} %multiply_convert_fusion), calls=%async_computation | async-start | bytes 2097152 | tf_op jit(solution)/shard_map/all_to_all | solution.py:124
  322.3 23.6 %copy-start.1 = (f32[64,16,32]{0,2,1:T(8,128)}, f32[64,16,32]{0,2,1:T(8,128)S(1)}, u32[]{:S(2)}) copy-start(f32[64,16,32]{0,2,1:T(8,128)S(1)} %multiply_add_fusion.7) | copy-start | bytes 393220
  347.1 3.4 copy-start.5
  371.6 2.5 copy-start.12
  374.2 5.1 copy-start.6
  378.2 3.5 copy-start.4
  379.3 2.2 copy-start.13
  381.6 11.7 %copy-start.3 = (f32[32,16,32]{0,2,1:T(8,128)S(1)}, f32[32,16,32]{0,2,1:T(8,128)}, u32[]{:S(2)}) copy-start(f32[32,16,32]{0,2,1:T(8,128)} %multiply_add_fusion.6) | copy-start | bytes 196612
  392.2 5.3 copy-start.2
  396.4 23.6 %copy-start.10 = (f32[63,16,32]{2,1,0:T(8,128)S(1)}, f32[63,16,32]{2,1,0:T(8,128)}, u32[]{:S(2)}) copy-start(f32[63,16,32]{2,1,0:T(8,128)} %slice.248) | copy-start | bytes 387076
  397.7 24.5 %slice-start = ((f32[128,16,32]{2,1,0:T(8,128)}), f32[1,16,32]{2,1,0:T(8,128)S(1)}, s32[]{:S(2)}) async-start(f32[128,16,32]{2,1,0:T(8,128)} %copy-done.7), calls=%async_computation.3 | async-start | bytes 16384 | tf_op jit(solution)/shard_map/slice | solution.py:77
  421.0 6.8 %copy-start.11 = (f32[128,16,32]{0,2,1:T(8,128)S(1)}, f32[128,16,32]{0,2,1:T(8,128)}, u32[]{:S(2)}) copy-start(f32[128,16,32]{0,2,1:T(8,128)} %pad.126) | copy-start | bytes 786436
  441.8 3.5 copy-start.8
  581.2 18.6 %all-to-all-start.1 = ((bf16[8,2048,32]{1,2,0:T(8,128)(2,1)}), bf16[8,2048,32]{1,2,0:T(8,128)(2,1)S(1)}, u32[]{:S(2)}, u32[]{:S(2)}) async-start(bf16[8,2048,32]{1,2,0:T(8,128)(2,1)} %copy.194), calls=%async_computation.1 | async-start | bytes 2097152 | tf_op jit(solution)/shard_map/all_to_all | solution.py:131
  584.8 15.0 %copy-start.18 = (f32[256]{0:T(256)S(1)}, f32[256]{0:T(256)}, u32[]{:S(2)}) copy-start(f32[256]{0:T(256)} %param.17) | copy-start | bytes 3076
  (2 other events, 1.7 us)
Sparse Core Ops, SparseCore 0:
  50.0 120.6 all-gather.1
where the time goes:
time: 617 us; the launch traced here: 613 us
  matrix products  196 us (32%)
  local copies, waits for them, and re-layouts  142 us (23%)
  waiting for transfers between devices  136 us (22%)
  other arithmetic  69.7 us (11%)
  blocking collectives  38.6 us (6%)
  starting transfers between devices  16.4 us (3%)
  between operations  14 us (2%)
    conv_general_dilated x2, matrix products, depthwise(): lax.conv_general_dilated(signal, kernel, (1,), ((front, 0),), dimension_n...  178 us
    all_gather x1, waiting for transfers between devices, on_device(): lax.all_gather(normed, 'chan', axis=1, tiled=True)  112 us
    slice x21, local copies, waits for them, and re-layouts, modal_local(): lax.associative_scan(combine_states, (step_decay, block_ends), axis=0)  44.4 us
    psum x1, blocking collectives, on_device(): squares = lax.psum(jnp.sum(values * values, axis=1), 'chan')  38.6 us
    unnamed x48, local copies, waits for them, and re-layouts  37.8 us
    pad x10, local copies, waits for them, and re-layouts, modal_local(): lax.associative_scan(combine_states, (step_decay, block_ends), axis=0)  28.4 us
    dot_general x1, matrix products, on_device(): jnp.dot(lax.all_gather(normed, 'chan', axis=1, tiled=True), flat_weight,...  18.2 us
    add x12, other arithmetic, combine_states(): return (earlier[0] * later[0], later[0] * earlier[1] + later[1])  14.2 us
  transfers between devices with their start and end apart: 5, of which 3 were waited for; matrix products, arithmetic and copies ran while one was open for 4% of the time, Pallas kernels for 0%

commit v1 on v0

v1 whole, which is shorter than its diff:
```python
import functools

import jax
import jax.numpy as jnp
from jax import lax
from jax.experimental import pallas as pl
from jax.experimental.pallas import tpu as pltpu
from jax.sharding import PartitionSpec as P

norm_epsilon = 1e-05
lanes = 128
segs = 8
steps = 32
chunk = segs * steps
taps = 128
back = taps // steps
block = 16
group = 8


def sublane():
    return lax.broadcasted_iota(jnp.int32, (segs, lanes), 0)


def fill(row):
    return jnp.broadcast_to(row, (segs, lanes))


def lane_tile(i):
    return slice(i * lanes, (i + 1) * lanes)


def set_constants(groups, modes, sf_ref, mr_ref, decay_ref, weight_ref, skip_ref, sfb, fb, lam, skb, pw):
    for g in range(groups):
        cols = lane_tile(g)
        for s in range(3):
            for j in range(3):
                sfb[(s * groups + g) * 3 + j] = fill(sf_ref[j, s : s + 1, cols])
        skb[g] = fill(skip_ref[:, cols])

        def taps_at(t, carry):
            rows = mr_ref[pl.ds(pl.multiple_of(t * 16, 16), 16), cols].astype(jnp.float32)
            for i in range(16):
                fb[g, t * 16 + i] = fill(rows[i : i + 1])
            return carry

        lax.fori_loop(0, taps // 16, taps_at, 0)
        at = sublane().astype(jnp.float32) * float(steps)
        for m in range(modes):
            d = fill(decay_ref[m : m + 1, cols])
            lam[0, g, m] = jnp.exp(-d)
            lam[1, g, m] = fill(weight_ref[m : m + 1, cols])
            pw[0, g, m] = jnp.exp(d * (-1.0 * steps))
            pw[1, g, m] = jnp.exp(d * (-2.0 * steps))
            pw[2, g, m] = jnp.exp(d * (-4.0 * steps))
            pw[3, g, m] = jnp.exp(d * (-8.0 * steps))
            pw[4, g, m] = jnp.exp(-d * at)


def strided(ref, lead, r):
    return ref[lead, pl.ds(r, segs, stride=steps), :]


def short_part(groups, pj, tail, sfb, qs, pe):
    sub = sublane()
    for g in range(groups):
        names = [s * groups + g for s in range(3)]
        old = []
        for n in names:
            last = strided(pj, n, steps - 1)
            before = strided(pj, n, steps - 2)
            turned = (pltpu.roll(last, 1, 0), pltpu.roll(before, 1, 0))
            old.append(
                (
                    jnp.where(sub == 0, tail[n, 0], turned[0]),
                    jnp.where(sub == 0, tail[n, 1], turned[1]),
                )
            )
            tail[n, 0] = turned[0]
            tail[n, 1] = turned[1]

        def step(r, carry):
            after, featured = [], []
            for n, (one, two) in zip(names, carry):
                now = strided(pj, n, r)
                featured.append(sfb[n * 3] * now + sfb[n * 3 + 1] * one + sfb[n * 3 + 2] * two)
                after.append((now, one))
            product = (featured[1] * featured[2]).astype(jnp.bfloat16).astype(jnp.float32)
            qs[g, r] = featured[0]
            past = pe[g, taps + r]
            for i in range(1, back + 1):
                pe[g, taps - steps * i + r] = pltpu.roll(
                    jnp.where(sub >= segs - i, past, product), i, 0
                )
            pe[g, taps + r] = product
            return tuple(after)

        lax.fori_loop(0, steps, step, tuple(old), unroll=4)


def medium_part(groups, pe, fb, qs, gs, ls):
    for g in range(groups):

        def at_block(b, carry):
            def taps_at(t, sums):
                base = taps + b * block - t * group
                window = [pe[g, base - group + 1 + i] for i in range(block + group - 1)]
                sums = list(sums)
                for j in range(group):
                    tap = fb[g, t * group + j]
                    for i in range(block):
                        sums[i] = sums[i] + tap * window[group - 1 + i - j]
                return tuple(sums)

            zero = jnp.zeros((segs, lanes), jnp.float32)
            sums = lax.fori_loop(0, taps // group, taps_at, (zero,) * block)
            for i in range(block):
                r = b * block + i
                mixed = (qs[g, r] * sums[i]).astype(jnp.bfloat16).astype(jnp.float32)
                gate = strided(gs, g, r)
                ls[g, r] = (gate * mixed).astype(jnp.bfloat16).astype(jnp.float32)
            return carry

        lax.fori_loop(0, steps // block, at_block, 0)


def long_part(groups, modes, k, ls, lam, skb, pw, carry_ref, ys, inits):
    sub = sublane()
    for g in range(groups):

        def step(r, states):
            value = ls[g, r]
            total = skb[g] * value
            after = []
            for m in range(modes):
                state = lam[0, g, m] * states[m] + value
                total = total + lam[1, g, m] * state
                after.append(state)
            ys[k, g, r] = total
            return tuple(after)

        zero = jnp.zeros((segs, lanes), jnp.float32)
        ends = lax.fori_loop(0, steps, step, (zero,) * modes, unroll=2)
        for m in range(modes):
            scan = ends[m]
            for n in range(3):
                scan = scan + jnp.where(
                    sub >= 1 << n, pw[n, g, m] * pltpu.roll(scan, 1 << n, 0), 0.0
                )
            carry = carry_ref[g, m]
            inits[k, g, m] = (
                jnp.where(sub == 0, 0.0, pltpu.roll(scan, 1, 0)) + pw[4, g, m] * carry
            )
            carry_ref[g, m] = fill(scan[segs - 1 : segs]) + pw[3, g, m] * carry


def finish_part(groups, modes, k, incoming, lam, pw, ys, inits, gs, outs):
    for g in range(groups):
        starts = []
        for m in range(modes):
            start = incoming[g, m]
            starts.append(lam[1, g, m] * (inits[k, g, m] + pw[4, g, m] * start))
            incoming[g, m] = pw[3, g, m] * start

        def step(r, states):
            total = ys[k, g, r]
            after = []
            for m in range(modes):
                state = lam[0, g, m] * states[m]
                total = total + state
                after.append(state)
            outs[g, pl.ds(r, segs, stride=steps), :] = strided(gs, g, r) * total
            return tuple(after)

        lax.fori_loop(0, steps, step, tuple(starts), unroll=2)


def load_gates(groups, which, k, gates_ref, gs):
    rows = pl.ds(pl.multiple_of(k * chunk, chunk), chunk)
    for g in range(groups):
        gs[g] = gates_ref[which, rows, lane_tile(g)].astype(jnp.float32)


def local_kernel(
    groups, modes, chunks,
    proj_ref, halo_ref, sf_ref, mr_ref, gates_ref, decay_ref, weight_ref, skip_ref,
    ys, inits, ends_ref,
    pj, tail, sfb, qs, pe, fb, gs, ls, lam, skb, pw, carry_ref,
):
    set_constants(groups, modes, sf_ref, mr_ref, decay_ref, weight_ref, skip_ref, sfb, fb, lam, skb, pw)
    carry_ref[...] = jnp.zeros_like(carry_ref)
    tail[...] = jnp.zeros_like(tail)
    pe[...] = jnp.zeros_like(pe)
    for n in range(3 * groups):
        pj[n] = halo_ref[:, lane_tile(n)].astype(jnp.float32)
    short_part(groups, pj, tail, sfb, qs, pe)

    def body(k, c):
        rows = pl.ds(pl.multiple_of(k * chunk, chunk), chunk)
        for n in range(3 * groups):
            pj[n] = proj_ref[rows, lane_tile(n)].astype(jnp.float32)
        short_part(groups, pj, tail, sfb, qs, pe)
        load_gates(groups, 1, k, gates_ref, gs)
        medium_part(groups, pe, fb, qs, gs, ls)
        long_part(groups, modes, k, ls, lam, skb, pw, carry_ref, ys, inits)
        return c

    lax.fori_loop(0, chunks, body, 0)
    for g in range(groups):
        for m in range(modes):
            ends_ref[g, m : m + 1, :] = carry_ref[g, m, 0:1, :]


def finish_kernel(
    groups, modes, chunks, peers,
    ends_ref, place_ref, ys, inits, gates_ref, decay_ref, weight_ref,
    out_ref,
    lam, pw, incoming, gs, outs,
):
    at = sublane().astype(jnp.float32) * float(steps)
    for g in range(groups):
        cols = lane_tile(g)
        for m in range(modes):
            d = fill(decay_ref[m : m + 1, cols])
            lam[0, g, m] = jnp.exp(-d)
            lam[1, g, m] = fill(weight_ref[m : m + 1, cols])
            pw[3, g, m] = jnp.exp(d * (-8.0 * steps))
            pw[4, g, m] = jnp.exp(-d * at)
        total = jnp.zeros((modes, lanes), jnp.float32)
        d = decay_ref[:, cols]
        for p in range(peers):
            gap = place_ref[p : p + 1, :]
            total = total + jnp.where(
                gap >= 0.0, jnp.exp(-d * (jnp.maximum(gap, 0.0) * float(chunk * chunks))), 0.0
            ) * ends_ref[p, g]
        for m in range(modes):
            incoming[g, m] = fill(total[m : m + 1])

    def body(k, c):
        load_gates(groups, 0, k, gates_ref, gs)
        finish_part(groups, modes, k, incoming, lam, pw, ys, inits, gs, outs)
        rows = pl.ds(pl.multiple_of(k * chunk, chunk), chunk)
        for g in range(groups):
            out_ref[rows, lane_tile(g)] = outs[g].astype(jnp.bfloat16)
        return c

    lax.fori_loop(0, chunks, body, 0)


def in_vmem(n):
    return [pl.BlockSpec(memory_space=pltpu.VMEM)] * n


def vregs(*lead):
    return pltpu.VMEM(lead + (segs, lanes), jnp.float32)


def local_call(proj, halo, short_filter, mr_filter, gates, decays, weights, skip):
    length = proj.shape[0]
    modes, width = decays.shape
    groups, chunks = width // lanes, length // chunk
    f32 = jnp.float32
    return pl.pallas_call(
        functools.partial(local_kernel, groups, modes, chunks),
        out_shape=(
            jax.ShapeDtypeStruct((chunks, groups, steps, segs, lanes), f32),
            jax.ShapeDtypeStruct((chunks, groups, modes, segs, lanes), f32),
            jax.ShapeDtypeStruct((groups, modes, lanes), f32),
        ),
        in_specs=in_vmem(8),
        out_specs=tuple(in_vmem(3)),
        scratch_shapes=[
            pltpu.VMEM((3 * groups, chunk, lanes), f32),
            vregs(3 * groups, 2),
            vregs(9 * groups),
            vregs(groups, steps),
            vregs(groups, taps + steps),
            vregs(groups, taps),
            pltpu.VMEM((groups, chunk, lanes), f32),
            vregs(groups, steps),
            vregs(2, groups, modes),
            vregs(groups),
            vregs(5, groups, modes),
            vregs(groups, modes),
        ],
        compiler_params=pltpu.CompilerParams(vmem_limit_bytes=56 << 20),
    )(proj, halo, short_filter, mr_filter, gates, decays, weights, skip)


def finish_call(ends, place, ys, inits, gates, decays, weights):
    chunks = ys.shape[0]
    modes, width = decays.shape
    groups = width // lanes
    return pl.pallas_call(
        functools.partial(finish_kernel, groups, modes, chunks, ends.shape[0]),
        out_shape=jax.ShapeDtypeStruct((chunks * chunk, width), jnp.bfloat16),
        in_specs=in_vmem(7),
        out_specs=pl.BlockSpec(memory_space=pltpu.VMEM),
        scratch_shapes=[
            vregs(2, groups, modes),
            vregs(5, groups, modes),
            vregs(groups, modes),
            pltpu.VMEM((groups, chunk, lanes), jnp.float32),
            pltpu.VMEM((groups, chunk, lanes), jnp.float32),
        ],
        compiler_params=pltpu.CompilerParams(vmem_limit_bytes=56 << 20),
    )(ends, place, ys, inits, gates, decays, weights)


def shifted(value, axis, by):
    peers = lax.axis_size(axis)
    pairs = [(i, i + by) for i in range(peers) if 0 <= i + by < peers]
    return lax.ppermute(value, axis, pairs)


def on_device(
    resid, norm_gain, feat_weight, short_filter, mr_filter, gates_lr, decay_rate, residue, skip_gain
):
    tokens, channels = resid.shape
    width = feat_weight.shape[0]
    values = resid.astype(jnp.float32)
    squares = lax.psum(jnp.sum(values * values, axis=1), "chan")
    inv_scale = lax.rsqrt(squares / width + norm_epsilon)
    normed = (values * inv_scale[:, None] * norm_gain.astype(jnp.float32)[None]).astype(jnp.bfloat16)
    rows = lax.all_gather(normed, "chan", axis=1, tiled=True)
    projected = jnp.concatenate(
        [
            jnp.dot(rows, feat_weight[:, s], preferred_element_type=jnp.float32).astype(jnp.bfloat16)
            for s in range(3)
        ],
        axis=1,
    )
    halo = shifted(projected[tokens - chunk :], "seq", 1)
    gates = jnp.transpose(gates_lr, (1, 0, 2))
    weights = residue * jnp.sqrt(-jnp.expm1(-2.0 * decay_rate))
    ys, inits, ends = local_call(
        projected, halo, short_filter, mr_filter, gates, decay_rate, weights, skip_gain[None]
    )
    all_ends = lax.all_gather(ends, "seq")
    peers = lax.axis_size("seq")
    gap = lax.axis_index("seq") - 1 - jnp.arange(peers)
    place = jnp.broadcast_to(gap.astype(jnp.float32)[:, None], (peers, lanes))
    return finish_call(all_ends, place, ys, inits, gates, decay_rate, weights)


def solution(mesh):
    in_specs = (
        P("seq", "chan"),
        P("chan"),
        P(None, None, "chan"),
        P(None, None, "chan"),
        P(None, "chan"),
        P("seq", None, "chan"),
        P(None, "chan"),
        P(None, "chan"),
        P("chan"),
    )
    return jax.shard_map(
        on_device, mesh=mesh, in_specs=in_specs, out_specs=P("seq", "chan"), check_vma=False
    )
```

time: 617 us -> 302 us (0.49)
  matrix products: 196 us -> 24.6 us
  local copies, waits for them, and re-layouts: 142 us -> 2.33 us
  other arithmetic: 69.7 us -> 6.37 us
  Pallas kernels: 0 us -> 53 us
  blocking collectives: 38.6 us -> 69.6 us
  starting transfers between devices: 16.4 us -> 4.53 us
  waiting for transfers between devices: 136 us -> 126 us
    conv_general_dilated x2 -> x0, matrix products: 178 us -> none  [depthwise(): lax.conv_general_dilated(signal, kernel, (1,), ((front, 0),), dimension_n...]
    pallas_call x0 -> x2, Pallas kernels: none -> 53 us  [the longest x1 42.1 us: local_call(): pl.pallas_call(functools.partial(local_kernel, groups, modes, chunks), ou...]
    slice x26 -> x1, local copies, waits for them, and re-layouts: 51.7 us -> 0.03 us  [on_device(): halo = shifted(projected[tokens - chunk:], 'seq', 1)]
    unnamed x48 -> x9, local copies, waits for them, and re-layouts: 37.8 us -> 1.65 us
    all_gather x0 -> x1, blocking collectives: none -> 31 us  [on_device(): all_ends = lax.all_gather(ends, 'seq')]
    pad x10 -> x0, local copies, waits for them, and re-layouts: 28.4 us -> none  [modal_local(): lax.associative_scan(combine_states, (step_decay, block_ends), axis=0)]
    add x21 -> x0, other arithmetic: 25.1 us -> none  [the longest x12 14.2 us: combine_states(): return (earlier[0] * later[0], later[0] * earlier[1] + later[1])]
    all_to_all x2 -> x0, waiting for transfers between devices: 23.5 us -> none  [the longest x1 12.4 us: on_device(): lax.all_to_all(as_sent(whole_conv), 'seq', split_axis=0, concat_axis=1, t...]
  transfers between devices with their start and end apart: 5 -> 2, of which waited for: 3 -> 2; matrix products, arithmetic and copies ran while one was open for 4% -> 1% of each run, Pallas kernels for 0% -> 0%
where the time goes in v1:
time: 302 us; the launch traced here: 300 us
  waiting for transfers between devices  126 us (42%)
  blocking collectives  69.6 us (23%)
  Pallas kernels  53 us (18%)
  matrix products  24.6 us (8%)
  between operations  13.5 us (4%)
  other arithmetic  6.37 us (2%)
  starting transfers between devices  4.53 us (2%)
    all_gather x1, waiting for transfers between devices, on_device(): rows = lax.all_gather(normed, 'chan', axis=1, tiled=True)  121 us
    pallas_call x1, Pallas kernels, local_call(): pl.pallas_call(functools.partial(local_kernel, groups, modes, chunks), ou...  42.1 us
    psum x1, blocking collectives, on_device(): squares = lax.psum(jnp.sum(values * values, axis=1), 'chan')  38.6 us
    all_gather x1, blocking collectives, on_device(): all_ends = lax.all_gather(ends, 'seq')  31 us
    dot_general x3, matrix products, on_device(): jnp.dot(rows, feat_weight[:, s], preferred_element_type=jnp.float32)  24.6 us
    pallas_call x1, Pallas kernels, finish_call(): pl.pallas_call(functools.partial(finish_kernel, groups, modes, chunks, en...  10.9 us
  transfers between devices with their start and end apart: 2, of which 2 were waited for; matrix products, arithmetic and copies ran while one was open for 1% of the time, Pallas kernels for 0%

profile of v1, /device:TPU:0, one launch (start us, length us, event | category | flops | bytes accessed | tf_op | source)
XLA Modules:
  0.0 299.7 jit_solution(3194902581969403459)
XLA Ops:
  6.5 0.0 all-gather.3.cloned.1.call-start
  6.5 1.6 fusion
  8.1 38.6 %psum.7 = f32[2048]{0:T(1024)S(1)} all-reduce(f32[2048]{0:T(1024)S(1)} %fusion), channel_id=1, replica_groups=mesh['seq'=8,'chan'=16] {'chan'}, use_global_device_ids=true, to_apply=%region_1.0 | all-reduce | flops 2048 | bytes 16384 | tf_op jit(solution)/shard_map/psum | solution.py:322
  46.7 0.7 convert_element_type.26
  47.4 2.5 fusion.2
  49.9 0.0 all-gather.3.cloned.1.call-update
  49.9 120.8 %all-gather.3.cloned.1.call-done = bf16[2048,4096]{1,0:T(8,128)(2,1)} async-done(((bf16[2048,256]{1,0:T(8,128)(2,1)}), bf16[2048,4096]{1,0:T(8,128)(2,1)}) %all-gather.3.cloned.1.call-update) | async-done | bytes 16777232 | tf_op jit(solution)/shard_map/all_gather | solution.py:325
  170.7 11.2 %convolution_convert_fusion = bf16[2048,256]{1,0:T(8,128)(2,1)S(1)} fusion(bf16[2048,4096]{1,0:T(8,128)(2,1)} %all-gather.3.cloned.1.call-done, bf16[4096,3,256]{2,0,1:T(8,128)(2,1)} %param.11), kind=kOutput, calls=%fused_computation.3 | convolution fusion | flops 4295491584 | bytes 19922944 | tf_op jit(solution)/shard_map/dot_general | solution.py:328
  181.9 0.0 copy-done.3
  181.9 6.6 %convolution_convert_fusion.1 = bf16[2048,256]{1,0:T(8,128)(2,1)S(1)} fusion(bf16[2048,4096]{1,0:T(8,128)(2,1)S(1)} %copy-done.3, bf16[4096,3,256]{2,0,1:T(8,128)(2,1)} %param.11), kind=kOutput, calls=%fused_computation.4 | convolution fusion | flops 4295491584 | bytes 19922944 | tf_op jit(solution)/shard_map/dot_general | solution.py:328
  188.5 6.8 %convolution_convert_fusion.2 = bf16[2048,256]{1,0:T(8,128)(2,1)S(1)} fusion(bf16[2048,4096]{1,0:T(8,128)(2,1)S(1)} %copy-done.3, bf16[4096,3,256]{2,0,1:T(8,128)(2,1)} %param.11), kind=kOutput, calls=%fused_computation.5 | convolution fusion | flops 4295491584 | bytes 19922944 | tf_op jit(solution)/shard_map/dot_general | solution.py:328
  195.3 0.0 copy-start.1
  195.3 0.3 pad_maximum_fusion.proj_ref
  195.6 0.0 copy-start.2
  195.7 4.5 %collective-permute-start = (bf16[256,768]{1,0:T(8,128)(2,1)S(1)}, bf16[256,768]{1,0:T(8,128)(2,1)}, u32[]{:S(2)}, u32[]{:S(2)}) collective-permute-start(bf16[256,768]{1,0:T(8,128)(2,1)S(1)} %slice.16), channel_id=1, source_target_pairs={{0,16},{16,32},{32,48},{48,64},{64,80},{80,96},{96,112},{1,17},{17... | collective-permute-start | bytes 1179656 | tf_op jit(solution)/shard_map/ppermute | solution.py:313
  200.2 0.0 copy-done.1
  200.2 1.6 copy.22
  201.8 1.3 sqrt_multiply_fusion.weight_ref
  203.2 5.0 %collective-permute-done.halo_ref = bf16[256,768]{1,0:T(8,128)(2,1)} collective-permute-done((bf16[256,768]{1,0:T(8,128)(2,1)S(1)}, bf16[256,768]{1,0:T(8,128)(2,1)}, u32[]{:S(2)}, u32[]{:S(2)}) %collective-permute-start) | collective-permute-done | bytes 393248 | tf_op jit(solution)/shard_map/ppermute | solution.py:313
  208.2 0.0 copy-done
  208.2 42.1 %shard_map.91 = (f32[8,2,32,8,128]{4,3,2,1,0:T(8,128)}, f32[8,2,16,8,128]{4,3,2,1,0:T(8,128)}, f32[2,16,128]{2,1,0:T(8,128)}) custom-call(bf16[2048,768]{1,0:T(8,128)(2,1)} %copy-done, bf16[256,768]{1,0:T(8,128)(2,1)} %collective-permute-done.halo_ref, f32[3,3,256]{2,1,0:T(4,128)} %sf_ref.1, bf16[128,256]{1,0:T(8,128)(2,1)} %mr_ref.1, ...), custom_call_target="tpu_custom_call" | custom-call | tf_op jit(solution)/shard_map/pallas_call | solution.py:263
  250.3 31.0 %all-gather = f32[16,16,128]{2,1,0:T(8,128)} all-gather(f32[2,16,128]{2,1,0:T(8,128)} %get-tuple-element.8), channel_id=2, replica_groups=mesh['seq'=8,'chan'=16] {'seq'}, dimensions={0}, use_global_device_ids=true | all-gather | bytes 147456 | tf_op jit(solution)/shard_map/all_gather | solution.py:339
  281.3 0.7 broadcast_in_dim.5.place_ref
  282.0 10.9 %shard_map.92 = bf16[2048,256]{1,0:T(8,128)(2,1)} custom-call(f32[8,2,16,128]{3,2,1,0:T(8,128)} %bitcast.19, f32[8,128]{1,0:T(8,128)} %broadcast_in_dim.5.place_ref, f32[8,2,32,8,128]{4,3,2,1,0:T(8,128)} %get-tuple-element.9.ys, f32[8,2,16,8,128]{4,3,2,1,0:T(8,128)} %get-tuple-element.10.inits, bf16[2,2048,256]{2,1,0:T(8,128)(2,1)} %bitcast.18, ...), custom_call_target="tpu_custom_call" | custom-call | tf_op jit(solution)/shard_map/pallas_call | solution.py:294
  (6 shorter events, 0.0 us)
Async XLA Ops:
  6.5 164.2 %all-gather.3.cloned.1.call-start = ((), (), s32[]{:S(2)}) async-start(), calls=%async_computation | async-start | bytes 17825792 | tf_op jit(solution)/shard_map/all_gather | solution.py:325
  170.7 11.2 %copy-start.3 = (bf16[2048,4096]{1,0:T(8,128)(2,1)S(1)}, bf16[2048,4096]{1,0:T(8,128)(2,1)}, u32[]{:S(2)}) copy-start(bf16[2048,4096]{1,0:T(8,128)(2,1)} %all-gather.3.cloned.1.call-done) | copy-start | bytes 50331652
  195.3 4.9 %copy-start.1 = (bf16[2048,2,256]{2,1,0:T(2,128)(2,1)S(1)}, bf16[2048,2,256]{2,1,0:T(2,128)(2,1)}, u32[]{:S(2)}) copy-start(bf16[2048,2,256]{2,1,0:T(2,128)(2,1)} %param.14) | copy-start | bytes 6291460
  195.6 12.6 %copy-start = (bf16[2048,768]{1,0:T(8,128)(2,1)}, bf16[2048,768]{1,0:T(8,128)(2,1)S(1)}, u32[]{:S(2)}) copy-start(bf16[2048,768]{1,0:T(8,128)(2,1)S(1)} %pad_maximum_fusion.proj_ref) | copy-start | bytes 9437188
  195.6 6.2 %copy-start.2 = (f32[16,256]{1,0:T(8,128)S(1)}, f32[16,256]{1,0:T(8,128)}, u32[]{:S(2)}) copy-start(f32[16,256]{1,0:T(8,128)} %decay_ref.3) | copy-start | bytes 49156
  195.7 12.5 %collective-permute-start = (bf16[256,768]{1,0:T(8,128)(2,1)S(1)}, bf16[256,768]{1,0:T(8,128)(2,1)}, u32[]{:S(2)}, u32[]{:S(2)}) collective-permute-start(bf16[256,768]{1,0:T(8,128)(2,1)S(1)} %slice.16), channel_id=1, source_target_pairs={{0,16},{16,32},{32,48},{48,64},{64,80},{80,96},{96,112},{1,17},{17... | collective-permute-start | bytes 1179656 | tf_op jit(solution)/shard_map/ppermute | solution.py:313
Sparse Core Ops, SparseCore 0:
  50.0 120.6 all-gather.2

commit v2 on v1

--- a/solution.py
+++ b/solution.py
@@ -181,62 +181,309 @@
         gs[g] = gates_ref[which, rows, lane_tile(g)].astype(jnp.float32)
 
 
-def local_kernel(
-    groups, modes, chunks,
-    proj_ref, halo_ref, sf_ref, mr_ref, gates_ref, decay_ref, weight_ref, skip_ref,
-    ys, inits, ends_ref,
-    pj, tail, sfb, qs, pe, fb, gs, ls, lam, skb, pw, carry_ref,
+MESH = pl.DeviceIdType.MESH
+kinds = 17
+halo_rows = taps + 16
+
+
+def columns(owner):
+    return pl.ds(pl.multiple_of(owner * 256, 256), 256)
+
+
+class Mover:
+    def __init__(self, chunks, resid_ref, rows_ref, send_sem, recv_sem, own_sem):
+        self.chunks = chunks
+        self.resid, self.rows = resid_ref, rows_ref
+        self.send_sem, self.recv_sem, self.own_sem = send_sem, recv_sem, own_sem
+        me = lax.axis_index("chan")
+        core, pair, x = lax.rem(me, 2), lax.rem(me // 2, 2), me // 4
+        right, left, far = lax.rem(x + 1, 4), lax.rem(x + 3, 4), lax.rem(x + 2, 4)
+        other = 1 - pair
+
+        def at(x, y):
+            return x * 4 + y * 2 + core
+
+        twin = x * 4 + pair * 2 + (1 - core)
+        self.me, self.twin = me, twin
+        whole, first, second = (0, chunk), (0, chunk // 2), (chunk // 2, chunk // 2)
+        here = [
+            at(x, pair), at(left, pair), at(right, pair), at(x, other),
+            at(far, pair), at(left, other), at(right, other), at(far, other),
+        ]
+        self.table = {
+            0: (at(right, pair), here[0], at(left, pair), whole),
+            1: (at(left, pair), here[0], at(right, pair), whole),
+            2: (at(x, other), here[0], at(x, other), whole),
+            3: (at(right, pair), at(left, pair), at(far, pair), first),
+            4: (at(left, pair), at(right, pair), at(far, pair), second),
+            5: (at(right, pair), at(x, other), at(left, other), whole),
+            6: (at(left, pair), at(x, other), at(right, other), whole),
+            7: (at(right, pair), at(left, other), at(far, other), first),
+            8: (at(left, pair), at(right, other), at(far, other), second),
+        }
+        flip = 1 - 2 * core
+        for n, block in enumerate(here):
+            self.table[9 + n] = (twin, block, block + flip, whole)
+
+    def token_rows(self, q):
+        return pl.ds(pl.multiple_of(lax.rem(q + self.chunks - 1, self.chunks) * chunk, chunk), chunk)
+
+    def make(self, q, kind):
+        target, sent, _, (begin, count) = self.table[kind]
+        place = self.rows.at[q, pl.ds(begin, count), columns(sent)]
+        source = self.resid.at[self.token_rows(q), :] if kind in (0, 1, 2, 9) else place
+        return pltpu.make_async_remote_copy(
+            src_ref=source,
+            dst_ref=place,
+            send_sem=self.send_sem.at[q, kind],
+            recv_sem=self.recv_sem.at[q, kind],
+            device_id={"chan": target},
+            device_id_type=MESH,
+        )
+
+    def start(self, q, *which):
+        for kind in which:
+            self.make(q, kind).start()
+
+    def sent(self, q):
+        for kind in range(kinds):
+            self.make(q, kind).wait_send()
+
+    def arrived(self, q, *which):
+        for kind in which:
+            target, _, received, (begin, count) = self.table[kind]
+            place = self.rows.at[q, pl.ds(begin, count), columns(received)]
+            pltpu.make_async_remote_copy(
+                src_ref=place,
+                dst_ref=place,
+                send_sem=self.send_sem.at[q, kind],
+                recv_sem=self.recv_sem.at[q, kind],
+                device_id={"chan": target},
+                device_id_type=MESH,
+            ).wait_recv()
+
+    def own(self, q):
+        return pltpu.make_async_copy(
+            self.resid.at[self.token_rows(q), :],
+            self.rows.at[q, :, columns(self.me)],
+            self.own_sem.at[q],
+        )
+
+    def stage_1(self, q):
+        self.start(q, 0, 1, 2, 9)
+        self.own(q).start()
+
+    def stage_2(self, q):
+        self.arrived(q, 2)
+        self.start(q, 5, 6, 12)
+        self.arrived(q, 0)
+        self.start(q, 3, 10)
+        self.arrived(q, 1)
+        self.start(q, 4, 11)
+
+    def stage_3(self, q):
+        self.arrived(q, 5)
+        self.start(q, 7, 14)
+        self.arrived(q, 6)
+        self.start(q, 8, 15)
+        self.arrived(q, 3, 4)
+        self.start(q, 13)
+
+    def stage_4(self, q):
+        self.arrived(q, 7, 8)
+        self.start(q, 16)
+
+    def stage_5(self, q):
+        self.own(q).wait()
+        self.arrived(q, 9, 10, 11, 12, 13, 14, 15, 16)
+
+
+def scale_weights(groups, peers, gains, wts):
+    def body(j, c):
+        for h in range(2):
+            row = gains[j, :, lane_tile(h)]
+            column = jnp.transpose(jnp.broadcast_to(row, (lanes, lanes)))
+            rows = pl.ds(pl.multiple_of(j * 256 + h * lanes, lanes), lanes)
+            for s in range(3):
+                for g in range(groups):
+                    value = wts[s, rows, lane_tile(g)].astype(jnp.float32)
+                    wts[s, rows, lane_tile(g)] = (value * column).astype(jnp.bfloat16)
+        return c
+
+    lax.fori_loop(0, peers, body, 0)
+
+
+def project(groups, q, width, rows_ref, wts, pj):
+    def square(t, total):
+        value = rows_ref[q, :, pl.ds(pl.multiple_of(t * lanes, lanes), lanes)].astype(jnp.float32)
+        return total + value * value
+
+    total = lax.fori_loop(
+        0, width // lanes, square, jnp.zeros((chunk, lanes), jnp.float32), unroll=2
+    )
+    scale = lax.rsqrt(jnp.sum(total, axis=1, keepdims=True) / width + norm_epsilon)
+    for s in range(3):
+        value = jnp.dot(rows_ref[q], wts[s], preferred_element_type=jnp.float32) * scale
+        value = value.astype(jnp.bfloat16).astype(jnp.float32)
+        for g in range(groups):
+            pj[s * groups + g] = value[:, lane_tile(g)]
+
+
+def fused_kernel(
+    groups, modes, chunks, sides, peers,
+    resid_ref, gain_ref, weight_hbm, sf_ref, mr_ref, gates_ref, decay_ref, modal_ref, skip_ref,
+    out_ref,
+    rows_ref, wts, gains, pj, pj_last, halo_out, halo_in, states, outs,
+    tail, sfb, qs, pe, fb, gs, ls, lam, skb, pw, carry_ref, incoming, ys, inits,
+    send_sem, recv_sem, own_sem, gain_send, gain_recv, state_send, state_recv, halo_sem, weight_sem,
 ):
-    set_constants(groups, modes, sf_ref, mr_ref, decay_ref, weight_ref, skip_ref, sfb, fb, lam, skb, pw)
+    me, part = lax.axis_index("chan"), lax.axis_index("seq")
+    load = pltpu.make_async_copy(weight_hbm, wts, weight_sem)
+    load.start()
+
+    barrier = pltpu.get_barrier_semaphore()
+    for o in range(1, sides):
+        pl.semaphore_signal(barrier, inc=1, device_id={"chan": lax.rem(me + o, sides)}, device_id_type=MESH)
+    for o in range(1, peers):
+        pl.semaphore_signal(barrier, inc=1, device_id={"seq": lax.rem(part + o, peers)}, device_id_type=MESH)
+    pl.semaphore_wait(barrier, sides + peers - 2)
+
+    mover = Mover(chunks, resid_ref, rows_ref, send_sem, recv_sem, own_sem)
+    mover.stage_1(0)
+
+    def gain_copy(o):
+        return pltpu.make_async_remote_copy(
+            src_ref=gain_ref, dst_ref=gains.at[me],
+            send_sem=gain_send.at[o], recv_sem=gain_recv.at[o],
+            device_id={"chan": lax.rem(me + o, sides)}, device_id_type=MESH,
+        )
+
+    for o in range(1, sides):
+        gain_copy(o).start()
+    mover.stage_1(1)
+    set_constants(groups, modes, sf_ref, mr_ref, decay_ref, modal_ref, skip_ref, sfb, fb, lam, skb, pw)
     carry_ref[...] = jnp.zeros_like(carry_ref)
     tail[...] = jnp.zeros_like(tail)
     pe[...] = jnp.zeros_like(pe)
-    for n in range(3 * groups):
-        pj[n] = halo_ref[:, lane_tile(n)].astype(jnp.float32)
-    short_part(groups, pj, tail, sfb, qs, pe)
-
-    def body(k, c):
-        rows = pl.ds(pl.multiple_of(k * chunk, chunk), chunk)
-        for n in range(3 * groups):
-            pj[n] = proj_ref[rows, lane_tile(n)].astype(jnp.float32)
-        short_part(groups, pj, tail, sfb, qs, pe)
-        load_gates(groups, 1, k, gates_ref, gs)
-        medium_part(groups, pe, fb, qs, gs, ls)
-        long_part(groups, modes, k, ls, lam, skb, pw, carry_ref, ys, inits)
+    mover.stage_2(0)
+    mover.stage_1(2)
+    mover.stage_2(1)
+    mover.stage_3(0)
+    own_gain = pltpu.make_async_copy(gain_ref, gains.at[me], weight_sem)
+    load.wait()
+    own_gain.start()
+    own_gain.wait()
+    for o in range(1, sides):
+        source = lax.rem(me + sides - o, sides)
+        pltpu.make_async_remote_copy(
+            src_ref=gain_ref, dst_ref=gains.at[source],
+            send_sem=gain_send.at[o], recv_sem=gain_recv.at[o],
+            device_id={"chan": source}, device_id_type=MESH,
+        ).wait_recv()
+    scale_weights(groups, sides, gains, wts)
+    mover.stage_1(3)
+    mover.stage_2(2)
+    mover.stage_3(1)
+    mover.stage_4(0)
+    mover.stage_1(4)
+
+    def halo_copy():
+        return pltpu.make_async_remote_copy(
+            src_ref=halo_out, dst_ref=halo_in,
+            send_sem=halo_sem.at[0], recv_sem=halo_sem.at[1],
+            device_id={"seq": lax.rem(part + 1, peers)}, device_id_type=MESH,
+        )
+
+    def body(q, c):
+        @pl.when(q < chunks)
+        def _():
+            mover.stage_5(q)
+
+        @pl.when(q + 1 < chunks)
+        def _():
+            mover.stage_4(q + 1)
+
+        @pl.when(q + 2 < chunks)
+        def _():
+            mover.stage_3(q + 2)
+
+        @pl.when(q < chunks)
+        def _():
+            project(groups, q, sides * 256, rows_ref, wts, pj)
+
+        @pl.when(q + 3 < chunks)
+        def _():
+            mover.stage_2(q + 3)
+
+        @pl.when(q + 5 < chunks)
+        def _():
+            mover.stage_1(q + 5)
+
+        @pl.when(q == 0)
+        def _():
+            for n in range(3 * groups):
+                pj_last[n] = pj[n]
+                halo_out[:, lane_tile(n)] = pj[n, chunk - halo_rows :, :].astype(jnp.bfloat16)
+            halo_copy().start()
+
+        @pl.when(q == 1)
+        def _():
+            halo_copy().wait()
+            seen = jnp.where(part > 0, 1.0, 0.0)
+            for n in range(3 * groups):
+                outs[n] = jnp.zeros((chunk, lanes), jnp.float32)
+                outs[n, chunk - halo_rows :, :] = halo_in[:, lane_tile(n)].astype(jnp.float32) * seen
+            short_part(groups, outs, tail, sfb, qs, pe)
+
+        @pl.when(q == chunks)
+        def _():
+            pj[...] = pj_last[...]
+
+        @pl.when(q > 0)
+        def _():
+            k = q - 1
+            short_part(groups, pj, tail, sfb, qs, pe)
+            load_gates(groups, 1, k, gates_ref, gs)
+            medium_part(groups, pe, fb, qs, gs, ls)
+            long_part(groups, modes, k, ls, lam, skb, pw, carry_ref, ys, inits)
+
         return c
 
-    lax.fori_loop(0, chunks, body, 0)
+    lax.fori_loop(0, chunks + 1, body, 0)
+
     for g in range(groups):
         for m in range(modes):
-            ends_ref[g, m : m + 1, :] = carry_ref[g, m, 0:1, :]
-
-
-def finish_kernel(
-    groups, modes, chunks, peers,
-    ends_ref, place_ref, ys, inits, gates_ref, decay_ref, weight_ref,
-    out_ref,
-    lam, pw, incoming, gs, outs,
-):
-    at = sublane().astype(jnp.float32) * float(steps)
-    for g in range(groups):
-        cols = lane_tile(g)
-        for m in range(modes):
-            d = fill(decay_ref[m : m + 1, cols])
-            lam[0, g, m] = jnp.exp(-d)
-            lam[1, g, m] = fill(weight_ref[m : m + 1, cols])
-            pw[3, g, m] = jnp.exp(d * (-8.0 * steps))
-            pw[4, g, m] = jnp.exp(-d * at)
+            states[0, g, m : m + 1, :] = carry_ref[g, m, 0:1, :]
+
+    def state_copy(o):
+        return pltpu.make_async_remote_copy(
+            src_ref=states.at[0], dst_ref=states.at[o],
+            send_sem=state_send.at[o], recv_sem=state_recv.at[o],
+            device_id={"seq": lax.rem(part + o, peers)}, device_id_type=MESH,
+        )
+
+    for o in range(1, peers):
+        state_copy(o).start()
+
+    def drain(q, c):
+        mover.sent(q)
+        return c
+
+    lax.fori_loop(0, chunks, drain, 0)
+    for o in range(1, sides):
+        gain_copy(o).wait_send()
+    for o in range(1, peers):
+        state_copy(o).wait()
+    for g in range(groups):
         total = jnp.zeros((modes, lanes), jnp.float32)
-        d = decay_ref[:, cols]
-        for p in range(peers):
-            gap = place_ref[p : p + 1, :]
-            total = total + jnp.where(
-                gap >= 0.0, jnp.exp(-d * (jnp.maximum(gap, 0.0) * float(chunk * chunks))), 0.0
-            ) * ends_ref[p, g]
+        d = decay_ref[:, lane_tile(g)]
+        for o in range(1, peers):
+            weight = jnp.exp(d * (-1.0 * chunk * chunks * (o - 1)))
+            total = total + jnp.where(part >= o, weight, 0.0) * states[o, g]
         for m in range(modes):
             incoming[g, m] = fill(total[m : m + 1])
 
-    def body(k, c):
+    def finish(k, c):
         load_gates(groups, 0, k, gates_ref, gs)
         finish_part(groups, modes, k, incoming, lam, pw, ys, inits, gs, outs)
         rows = pl.ds(pl.multiple_of(k * chunk, chunk), chunk)
@@ -244,7 +491,7 @@
             out_ref[rows, lane_tile(g)] = outs[g].astype(jnp.bfloat16)
         return c
 
-    lax.fori_loop(0, chunks, body, 0)
+    lax.fori_loop(0, chunks, finish, 0)
 
 
 def in_vmem(n):
@@ -255,21 +502,29 @@
     return pltpu.VMEM(lead + (segs, lanes), jnp.float32)
 
 
-def local_call(proj, halo, short_filter, mr_filter, gates, decays, weights, skip):
-    length = proj.shape[0]
-    modes, width = decays.shape
+def fused_call(resid, gain, weight, short_filter, mr_filter, gates, decays, modal, skip):
+    length, width = resid.shape
+    modes = decays.shape[0]
     groups, chunks = width // lanes, length // chunk
-    f32 = jnp.float32
+    sides, peers = lax.axis_size("chan"), lax.axis_size("seq")
+    f32, bf16 = jnp.float32, jnp.bfloat16
+    dma = pltpu.SemaphoreType.DMA
+    anywhere = pl.BlockSpec(memory_space=pl.ANY)
+    vmem = pl.BlockSpec(memory_space=pltpu.VMEM)
     return pl.pallas_call(
-        functools.partial(local_kernel, groups, modes, chunks),
-        out_shape=(
-            jax.ShapeDtypeStruct((chunks, groups, steps, segs, lanes), f32),
-            jax.ShapeDtypeStruct((chunks, groups, modes, segs, lanes), f32),
-            jax.ShapeDtypeStruct((groups, modes, lanes), f32),
-        ),
-        in_specs=in_vmem(8),
-        out_specs=tuple(in_vmem(3)),
+        functools.partial(fused_kernel, groups, modes, chunks, sides, peers),
+        out_shape=jax.ShapeDtypeStruct((length, width), bf16),
+        in_specs=[anywhere, vmem, anywhere] + [vmem] * 6,
+        out_specs=vmem,
         scratch_shapes=[
+            pltpu.VMEM((chunks, chunk, sides * width), bf16),
+            pltpu.VMEM((3, sides * width, width), bf16),
+            pltpu.VMEM((sides, 1, width), f32),
+            pltpu.VMEM((3 * groups, chunk, lanes), f32),
+            pltpu.VMEM((3 * groups, chunk, lanes), f32),
+            pltpu.VMEM((halo_rows, 3 * width), bf16),
+            pltpu.VMEM((halo_rows, 3 * width), bf16),
+            pltpu.VMEM((peers, groups, modes, lanes), f32),
             pltpu.VMEM((3 * groups, chunk, lanes), f32),
             vregs(3 * groups, 2),
             vregs(9 * groups),
@@ -282,65 +537,40 @@
             vregs(groups),
             vregs(5, groups, modes),
             vregs(groups, modes),
+            vregs(groups, modes),
+            vregs(chunks, groups, steps),
+            vregs(chunks, groups, modes),
+            dma((chunks, kinds)),
+            dma((chunks, kinds)),
+            dma((chunks,)),
+            dma((sides,)),
+            dma((sides,)),
+            dma((peers,)),
+            dma((peers,)),
+            dma((2,)),
+            dma,
         ],
-        compiler_params=pltpu.CompilerParams(vmem_limit_bytes=56 << 20),
-    )(proj, halo, short_filter, mr_filter, gates, decays, weights, skip)
-
-
-def finish_call(ends, place, ys, inits, gates, decays, weights):
-    chunks = ys.shape[0]
-    modes, width = decays.shape
-    groups = width // lanes
-    return pl.pallas_call(
-        functools.partial(finish_kernel, groups, modes, chunks, ends.shape[0]),
-        out_shape=jax.ShapeDtypeStruct((chunks * chunk, width), jnp.bfloat16),
-        in_specs=in_vmem(7),
-        out_specs=pl.BlockSpec(memory_space=pltpu.VMEM),
-        scratch_shapes=[
-            vregs(2, groups, modes),
-            vregs(5, groups, modes),
-            vregs(groups, modes),
-            pltpu.VMEM((groups, chunk, lanes), jnp.float32),
-            pltpu.VMEM((groups, chunk, lanes), jnp.float32),
-        ],
-        compiler_params=pltpu.CompilerParams(vmem_limit_bytes=56 << 20),
-    )(ends, place, ys, inits, gates, decays, weights)
-
-
-def shifted(value, axis, by):
-    peers = lax.axis_size(axis)
-    pairs = [(i, i + by) for i in range(peers) if 0 <= i + by < peers]
-    return lax.ppermute(value, axis, pairs)
+        compiler_params=pltpu.CompilerParams(
+            vmem_limit_bytes=60 << 20, collective_id=0, has_side_effects=True
+        ),
+    )(resid, gain, weight, short_filter, mr_filter, gates, decays, modal, skip)
 
 
 def on_device(
     resid, norm_gain, feat_weight, short_filter, mr_filter, gates_lr, decay_rate, residue, skip_gain
 ):
-    tokens, channels = resid.shape
-    width = feat_weight.shape[0]
-    values = resid.astype(jnp.float32)
-    squares = lax.psum(jnp.sum(values * values, axis=1), "chan")
-    inv_scale = lax.rsqrt(squares / width + norm_epsilon)
-    normed = (values * inv_scale[:, None] * norm_gain.astype(jnp.float32)[None]).astype(jnp.bfloat16)
-    rows = lax.all_gather(normed, "chan", axis=1, tiled=True)
-    projected = jnp.concatenate(
-        [
-            jnp.dot(rows, feat_weight[:, s], preferred_element_type=jnp.float32).astype(jnp.bfloat16)
-            for s in range(3)
-        ],
-        axis=1,
+    modal = residue * jnp.sqrt(-jnp.expm1(-2.0 * decay_rate))
+    return fused_call(
+        resid,
+        norm_gain.astype(jnp.float32)[None],
+        jnp.transpose(feat_weight, (1, 0, 2)),
+        short_filter,
+        mr_filter,
+        jnp.transpose(gates_lr, (1, 0, 2)),
+        decay_rate,
+        modal,
+        skip_gain[None],
     )
-    halo = shifted(projected[tokens - chunk :], "seq", 1)
-    gates = jnp.transpose(gates_lr, (1, 0, 2))
-    weights = residue * jnp.sqrt(-jnp.expm1(-2.0 * decay_rate))
-    ys, inits, ends = local_call(
-        projected, halo, short_filter, mr_filter, gates, decay_rate, weights, skip_gain[None]
-    )
-    all_ends = lax.all_gather(ends, "seq")
-    peers = lax.axis_size("seq")
-    gap = lax.axis_index("seq") - 1 - jnp.arange(peers)
-    place = jnp.broadcast_to(gap.astype(jnp.float32)[:, None], (peers, lanes))
-    return finish_call(all_ends, place, ys, inits, gates, decay_rate, weights)
 
 
 def solution(mesh):

time: 302 us -> 135 us (0.45)
  waiting for transfers between devices: 126 us -> 0 us
  Pallas kernels: 53 us -> 126 us
  blocking collectives: 69.6 us -> 0 us
  matrix products: 24.6 us -> 0 us
  between operations: 13.5 us -> 0.01 us
  starting transfers between devices: 4.53 us -> 0 us
  other arithmetic: 6.37 us -> 2.6 us
  local copies, waits for them, and re-layouts: 2.33 us -> 5.48 us
    all_gather x1 -> x0, waiting for transfers between devices: 121 us -> none  [on_device(): rows = lax.all_gather(normed, 'chan', axis=1, tiled=True)]
    pallas_call x2 -> x1, Pallas kernels: 53 us -> 126 us  [fused_call(): pl.pallas_call(functools.partial(fused_kernel, groups, modes, chunks, sid...]
    psum x1 -> x0, blocking collectives: 38.6 us -> none  [on_device(): squares = lax.psum(jnp.sum(values * values, axis=1), 'chan')]
    all_gather x1 -> x0, blocking collectives: 31 us -> none  [on_device(): all_ends = lax.all_gather(ends, 'seq')]
    dot_general x3 -> x0, matrix products: 24.6 us -> none  [on_device(): jnp.dot(rows, feat_weight[:, s], preferred_element_type=jnp.float32)]
    ppermute x1 -> x0, waiting for transfers between devices: 5.01 us -> none  [shifted(): return lax.ppermute(value, axis, pairs)]
    ppermute x1 -> x0, starting transfers between devices: 4.53 us -> none  [shifted(): return lax.ppermute(value, axis, pairs)]
    unnamed x9 -> x2, local copies, waits for them, and re-layouts: 1.65 us -> 5.48 us
  transfers between devices with their start and end apart: 2 -> 0, of which waited for: 2 -> 0; matrix products, arithmetic and copies ran while one was open for 1% -> 0% of each run, Pallas kernels for 0% -> 0%
where the time goes in v2:
time: 135 us; the launch traced here: 134 us
  Pallas kernels  126 us (93%)
  local copies, waits for them, and re-layouts  5.48 us (4%)
  other arithmetic  2.6 us (2%)
    pallas_call x1, Pallas kernels, fused_call(): pl.pallas_call(functools.partial(fused_kernel, groups, modes, chunks, sid...  126 us
    unnamed x2, local copies, waits for them, and re-layouts  5.48 us

profile of v2, /device:TPU:0, one launch (start us, length us, event | category | flops | bytes accessed | tf_op | source)
XLA Modules:
  0.0 134.4 jit_solution(12825095018911668485)
XLA Ops:
  0.0 1.2 broadcast_in_dim.11
  1.2 1.4 %sqrt_multiply_fusion.modal_ref = f32[16,256]{1,0:T(8,128)} fusion(f32[16,256]{1,0:T(8,128)} %param.16, f32[16,256]{1,0:T(8,128)} %decay_ref.1), kind=kLoop, calls=%fused_computation.1 | loop fusion | flops 12288 | bytes 49152 | tf_op jit(solution)/shard_map/mul | solution.py:562
  2.6 3.2 %copy.12 = bf16[2048,2,256]{2,0,1:T(8,128)(2,1)} copy(bf16[2048,2,256]{2,1,0:T(2,128)(2,1)} %param.14) | data formatting | bytes 4194304 | tf_op args[5]
  5.8 126.4 %shard_map.91 = bf16[2048,256]{1,0:T(8,128)(2,1)} custom-call(bf16[2048,256]{1,0:T(8,128)(2,1)} %resid_ref.1, f32[1,256]{1,0:T(1,128)} %bitcast.9, bf16[3,4096,256]{2,1,0:T(8,128)(2,1)} %bitcast.7, f32[3,3,256]{2,1,0:T(4,128)} %sf_ref.1, bf16[128,256]{1,0:T(8,128)(2,1)} %mr_ref.1, bf16[2,2048,256]{2,1,0:T(8,128)(2,1)} %bitcast.6, f32[16,256]{1,0:T(8,128)} %decay_ref.1, ...), custom_call_target="tpu_custom_call" | custom-call | tf_op jit(solution)/shard_map/pallas_call | solution.py:514
  132.2 2.3 %copy.14 = bf16[2048,256]{1,0:T(8,128)(2,1)} copy(bf16[2048,256]{1,0:T(8,128)(2,1)} %shard_map.91) | data formatting | bytes 2097152

commit v3 on v2

v3 whole, which is shorter than its diff:
```python
import functools

import jax
import jax.numpy as jnp
from jax import lax
from jax.experimental import pallas as pl
from jax.experimental.pallas import tpu as pltpu
from jax.sharding import PartitionSpec as P

norm_epsilon = 1e-05
lanes = 128
segs = 8
steps = 32
chunk = segs * steps
taps = 128
back = taps // steps
block = 16
group = 8


def sublane():
    return lax.broadcasted_iota(jnp.int32, (segs, lanes), 0)


def fill(row):
    return jnp.broadcast_to(row, (segs, lanes))


def lane_tile(i):
    return slice(i * lanes, (i + 1) * lanes)


def modal_weights(decay, residue):
    x = decay * 2.0
    small = x * (1.0 - x / 2.0 * (1.0 - x / 3.0 * (1.0 - x / 4.0 * (1.0 - x / 5.0 * (1.0 - x / 6.0)))))
    return residue * jnp.sqrt(jnp.where(x < 0.125, small, 1.0 - jnp.exp(-x)))


def set_constants(groups, modes, sf_ref, mr_ref, decay_ref, residue_ref, skip, sfb, fb, lam, skb, pw):
    for g in range(groups):
        cols = lane_tile(g)
        for s in range(3):
            for j in range(3):
                sfb[(s * groups + g) * 3 + j] = fill(sf_ref[j, s : s + 1, cols])
        skb[g] = fill(skip[:, cols])

        def taps_at(t, carry):
            rows = mr_ref[pl.ds(pl.multiple_of(t * 16, 16), 16), cols].astype(jnp.float32)
            for i in range(16):
                fb[g, t * 16 + i] = fill(rows[i : i + 1])
            return carry

        lax.fori_loop(0, taps // 16, taps_at, 0)
        at = sublane().astype(jnp.float32) * float(steps)
        modal = modal_weights(decay_ref[:, cols], residue_ref[:, cols])
        for m in range(modes):
            d = fill(decay_ref[m : m + 1, cols])
            lam[0, g, m] = jnp.exp(-d)
            lam[1, g, m] = fill(modal[m : m + 1])
            pw[0, g, m] = jnp.exp(d * (-1.0 * steps))
            pw[1, g, m] = jnp.exp(d * (-2.0 * steps))
            pw[2, g, m] = jnp.exp(d * (-4.0 * steps))
            pw[3, g, m] = jnp.exp(d * (-8.0 * steps))
            pw[4, g, m] = jnp.exp(-d * at)


def strided(ref, lead, r):
    return ref[lead, pl.ds(r, segs, stride=steps), :]


def short_part(groups, pj, tail, sfb, qs, pe):
    sub = sublane()
    for g in range(groups):
        names = [s * groups + g for s in range(3)]
        old = []
        for n in names:
            last = strided(pj, n, steps - 1)
            before = strided(pj, n, steps - 2)
            turned = (pltpu.roll(last, 1, 0), pltpu.roll(before, 1, 0))
            old.append(
                (
                    jnp.where(sub == 0, tail[n, 0], turned[0]),
                    jnp.where(sub == 0, tail[n, 1], turned[1]),
                )
            )
            tail[n, 0] = turned[0]
            tail[n, 1] = turned[1]

        def step(r, carry):
            after, featured = [], []
            for n, (one, two) in zip(names, carry):
                now = strided(pj, n, r)
                featured.append(sfb[n * 3] * now + sfb[n * 3 + 1] * one + sfb[n * 3 + 2] * two)
                after.append((now, one))
            product = (featured[1] * featured[2]).astype(jnp.bfloat16).astype(jnp.float32)
            qs[g, r] = featured[0]
            past = pe[g, taps + r]
            for i in range(1, back + 1):
                pe[g, taps - steps * i + r] = pltpu.roll(
                    jnp.where(sub >= segs - i, past, product), i, 0
                )
            pe[g, taps + r] = product
            return tuple(after)

        lax.fori_loop(0, steps, step, tuple(old), unroll=4)


def medium_part(groups, pe, fb, qs, gs, ls):
    for g in range(groups):

        def at_block(b, carry):
            def taps_at(t, sums):
                base = taps + b * block - t * group
                window = [pe[g, base - group + 1 + i] for i in range(block + group - 1)]
                sums = list(sums)
                for j in range(group):
                    tap = fb[g, t * group + j]
                    for i in range(block):
                        sums[i] = sums[i] + tap * window[group - 1 + i - j]
                return tuple(sums)

            zero = jnp.zeros((segs, lanes), jnp.float32)
            sums = lax.fori_loop(0, taps // group, taps_at, (zero,) * block)
            for i in range(block):
                r = b * block + i
                mixed = (qs[g, r] * sums[i]).astype(jnp.bfloat16).astype(jnp.float32)
                gate = gate_at(gs, groups, g, 1, r)
                ls[g, r] = (gate * mixed).astype(jnp.bfloat16).astype(jnp.float32)
            return carry

        lax.fori_loop(0, steps // block, at_block, 0)


def long_part(groups, modes, k, ls, lam, skb, pw, carry_ref, ys, inits):
    sub = sublane()
    for g in range(groups):

        def step(r, states):
            value = ls[g, r]
            total = skb[g] * value
            after = []
            for m in range(modes):
                state = lam[0, g, m] * states[m] + value
                total = total + lam[1, g, m] * state
                after.append(state)
            ys[k, g, r] = total
            return tuple(after)

        zero = jnp.zeros((segs, lanes), jnp.float32)
        ends = lax.fori_loop(0, steps, step, (zero,) * modes, unroll=2)
        for m in range(modes):
            scan = ends[m]
            for n in range(3):
                scan = scan + jnp.where(
                    sub >= 1 << n, pw[n, g, m] * pltpu.roll(scan, 1 << n, 0), 0.0
                )
            carry = carry_ref[g, m]
            inits[k, g, m] = (
                jnp.where(sub == 0, 0.0, pltpu.roll(scan, 1, 0)) + pw[4, g, m] * carry
            )
            carry_ref[g, m] = fill(scan[segs - 1 : segs]) + pw[3, g, m] * carry


def finish_part(groups, modes, k, incoming, lam, pw, ys, inits, gs, outs):
    for g in range(groups):
        starts = []
        for m in range(modes):
            start = incoming[g, m]
            starts.append(lam[1, g, m] * (inits[k, g, m] + pw[4, g, m] * start))
            incoming[g, m] = pw[3, g, m] * start

        def step(r, states):
            total = ys[k, g, r]
            after = []
            for m in range(modes):
                state = lam[0, g, m] * states[m]
                total = total + state
                after.append(state)
            outs[g, pl.ds(r, segs, stride=steps), :] = gate_at(gs, groups, g, 0, r) * total
            return tuple(after)

        lax.fori_loop(0, steps, step, tuple(starts), unroll=2)


def load_gates(k, gates, gs):
    rows = chunk * 4
    gs[...] = gates[pl.ds(pl.multiple_of(k * rows, rows), rows), :].astype(jnp.float32)


def gate_at(gs, groups, g, which, r):
    return gs[pl.ds((r * groups + g) * 2 + which, segs, stride=steps * groups * 2), :]


MESH = pl.DeviceIdType.MESH
kinds = 10
waits = 8
halo_rows = taps + 16
unit = 128
part_rows = 24


def place_of(owner):
    return lax.rem(owner, 2) * 8 + lax.rem(owner // 2, 2) * 4 + owner // 4


class Mover:
    def __init__(self, units, resid_ref, own_rows, rows_ref, send_sem, recv_sem, own_sem):
        self.units = units
        self.resid, self.own_rows, self.rows = resid_ref, own_rows, rows_ref
        self.send_sem, self.recv_sem, self.own_sem = send_sem, recv_sem, own_sem
        me = lax.axis_index("chan")
        core, pair, x = lax.rem(me, 2), lax.rem(me // 2, 2), me // 4
        right, left, far = lax.rem(x + 1, 4), lax.rem(x + 3, 4), lax.rem(x + 2, 4)
        other = 1 - pair

        def block(x, y):
            return core * 8 + y * 4 + x

        def device(x, y):
            return x * 4 + y * 2 + core

        self.here = block(x, pair)
        whole, first, second = (0, unit), (0, unit // 2), (unit // 2, unit // 2)
        east, west, across = device(right, pair), device(left, pair), device(x, other)
        twin = me + 1 - 2 * core
        self.table = (
            (east, block(x, pair), whole, 1, 0),
            (west, block(x, pair), whole, 1, 1),
            (across, block(x, pair), whole, 1, 2),
            (east, block(left, pair), first, 1, 3),
            (west, block(right, pair), second, 1, 3),
            (east, block(x, other), whole, 1, 4),
            (west, block(x, other), whole, 1, 5),
            (across, block(far, pair), whole, 1, 6),
            (twin, block(0, pair), whole, 4, 7),
            (twin, block(0, other), whole, 4, 7),
        )
        self.landing = (
            (block(left, pair), 1),
            (block(right, pair), 1),
            (block(x, other), 1),
            (block(far, pair), 1),
            (block(left, other), 1),
            (block(right, other), 1),
            (block(far, other), 1),
            ((1 - core) * 8, 8),
        )
        self.twin = twin

    def token_rows(self, q):
        first = lax.rem(q + self.units - chunk // unit, self.units)
        return pl.ds(pl.multiple_of(first * unit, unit), unit)

    def place(self, q, begin, count, owner, blocks):
        rows = pl.ds(pl.multiple_of(lax.rem(q, chunk // unit) * unit + begin, count), count)
        cols = pl.ds(pl.multiple_of(owner * 256, 256), blocks * 256)
        return self.rows.at[q // (chunk // unit), rows, cols]

    def remote(self, source, target_ref, kind, q, wait, target):
        return pltpu.make_async_remote_copy(
            src_ref=source,
            dst_ref=target_ref,
            send_sem=self.send_sem.at[kind],
            recv_sem=self.recv_sem.at[q, wait],
            device_id={"chan": target},
            device_id_type=MESH,
        )

    def start(self, q, *which):
        for kind in which:
            target, sent, (begin, count), blocks, wait = self.table[kind]
            place = self.place(q, begin, count, sent, blocks)
            source = self.resid.at[self.token_rows(q), :] if kind < 3 else place
            self.remote(source, place, kind, q, wait, target).start()

    def sent(self):
        for kind in range(kinds):
            _, _, (_, count), blocks, _ = self.table[kind]
            if blocks == 1:
                whole = self.own_rows.at[pl.ds(0, self.units * count), :]
            else:
                whole = self.rows.at[:, :, pl.ds(0, blocks * 256)]
            self.remote(whole, whole, kind, 0, 0, self.twin).wait_send()

    def arrived(self, q, *which):
        for wait in which:
            owner, blocks = self.landing[wait]
            place = self.place(q, 0, unit, owner, blocks)
            self.remote(place, place, 0, q, wait, self.twin).wait_recv()

    def own(self, q):
        return pltpu.make_async_copy(
            self.resid.at[self.token_rows(q), :],
            self.place(q, 0, unit, self.here, 1),
            self.own_sem.at[q],
        )

    def stage_1(self, q):
        self.start(q, 0, 1, 2)
        self.own(q).start()

    def stage_2(self, q):
        self.arrived(q, 2)
        self.start(q, 5, 6)
        self.arrived(q, 0)
        self.start(q, 3)
        self.arrived(q, 1)
        self.start(q, 4)

    def stage_3(self, q):
        self.own(q).wait()
        self.arrived(q, 3)
        self.start(q, 7, 8)

    def stage_4(self, q):
        self.arrived(q, 4, 5, 6)
        self.start(q, 9)

    def stage_5(self, q):
        self.arrived(q, 7)

    def tick(self, t):
        stages = ((4, self.stage_3), (6, self.stage_2), (8, self.stage_1), (3, self.stage_4))
        for lead, stage in stages:
            if isinstance(t, int):
                if 0 <= t + lead < self.units:
                    stage(t + lead)
            else:
                pl.when(t + lead < self.units)(functools.partial(stage, t + lead))


def scale_weights(groups, peers, parts, wts):
    def body(j, c):
        for h in range(2):
            row = parts[j, 16 + h : 17 + h, :]
            column = jnp.transpose(jnp.broadcast_to(row, (lanes, lanes)))
            rows = pl.ds(pl.multiple_of(j * 256 + h * lanes, lanes), lanes)
            for s in range(3):
                for g in range(groups):
                    value = wts[s, rows, lane_tile(g)].astype(jnp.float32)
                    wts[s, rows, lane_tile(g)] = (value * column).astype(jnp.bfloat16)
        return c

    lax.fori_loop(0, peers, body, 0)


def square_rows(tokens, own_rows, parts, me):
    def body(i, c):
        value = own_rows[pl.ds(pl.multiple_of(i * lanes, lanes), lanes), :].astype(jnp.float32)
        total = jnp.zeros((lanes, lanes), jnp.float32)
        for g in range(value.shape[1] // lanes):
            total = total + value[:, lane_tile(g)] * value[:, lane_tile(g)]
        parts[me, pl.ds(i, 1), :] = jnp.sum(jnp.transpose(total), axis=0, keepdims=True)
        return c

    lax.fori_loop(0, tokens // lanes, body, 0)


def project(groups, q, first, rows_ref, wts, scales, pj):
    columns_of = [
        jnp.transpose(jnp.broadcast_to(scales[pl.ds(first + h, 1), :], (lanes, lanes)))
        for h in range(chunk // lanes)
    ]
    for s in range(3):
        value = jnp.dot(rows_ref[q], wts[s], preferred_element_type=jnp.float32)
        for g in range(groups):
            for h, scale in enumerate(columns_of):
                piece = value[lane_tile(h), lane_tile(g)] * scale
                pj[s * groups + g, lane_tile(h), :] = piece.astype(jnp.bfloat16).astype(jnp.float32)


def fused_kernel(
    groups, modes, chunks, sides, peers,
    resid_ref, weight_hbm, gates_hbm, gain_ref, sf_ref, mr_ref, decay_ref, residue_ref, skip_ref,
    out_ref,
    rows_ref, wts, gates, own_rows, parts, scales, pj, pj_last, halo_out, halo_in, states, outs,
    tail, sfb, qs, pe, fb, gs, ls, lam, skb, pw, carry_ref, incoming, ys, inits,
    send_sem, recv_sem, own_sem, gain_send, gain_recv, state_send, state_recv, halo_sem, weight_sem, own_load_sem, gates_sem,
):
    me, part = lax.axis_index("chan"), lax.axis_index("seq")
    own_load = pltpu.make_async_copy(resid_ref, own_rows, own_load_sem)
    own_load.start()
    load = pltpu.make_async_copy(weight_hbm, wts, weight_sem)
    for p in range(sides):
        owner = (p % 4) * 4 + (p % 8 // 4) * 2 + p // 8
        pltpu.make_async_copy(
            weight_hbm.at[:, owner * 256 : (owner + 1) * 256, :],
            wts.at[:, p * 256 : (p + 1) * 256, :],
            weight_sem,
        ).start()
    gates_load = pltpu.make_async_copy(gates_hbm, gates, gates_sem)
    gates_load.start()

    barrier = pltpu.get_barrier_semaphore()
    for o in range(1, sides):
        pl.semaphore_signal(barrier, inc=1, device_id={"chan": lax.rem(me + o, sides)}, device_id_type=MESH)
    for o in range(1, peers):
        pl.semaphore_signal(barrier, inc=1, device_id={"seq": lax.rem(part + o, peers)}, device_id_type=MESH)
    pl.semaphore_wait(barrier, sides + peers - 2)

    units = chunks * chunk // unit
    mover = Mover(units, resid_ref, own_rows, rows_ref, send_sem, recv_sem, own_sem)
    mover.tick(-8)
    mover.tick(-7)

    gain = gain_ref[...].reshape(1, 256).astype(jnp.float32)
    parts[mover.here, 16:17, :] = gain[:, lane_tile(0)]
    parts[mover.here, 17:18, :] = gain[:, lane_tile(1)]
    own_load.wait()
    square_rows(chunks * chunk, own_rows, parts, mover.here)
    mover.tick(-6)
    skip = skip_ref[...].reshape(1, 256)
    set_constants(groups, modes, sf_ref, mr_ref, decay_ref, residue_ref, skip, sfb, fb, lam, skb, pw)

    def part_copy(o):
        return pltpu.make_async_remote_copy(
            src_ref=parts.at[mover.here], dst_ref=parts.at[mover.here],
            send_sem=gain_send.at[o], recv_sem=gain_recv.at[o],
            device_id={"chan": lax.rem(me + o, sides)}, device_id_type=MESH,
        )

    for o in range(1, sides):
        part_copy(o).start()
    mover.tick(-5)
    carry_ref[...] = jnp.zeros_like(carry_ref)
    tail[...] = jnp.zeros_like(tail)
    pe[...] = jnp.zeros_like(pe)
    load.wait()
    mover.tick(-4)
    for o in range(1, sides):
        source = lax.rem(me + sides - o, sides)
        pltpu.make_async_remote_copy(
            src_ref=parts.at[place_of(source)], dst_ref=parts.at[place_of(source)],
            send_sem=gain_send.at[o], recv_sem=gain_recv.at[o],
            device_id={"chan": source}, device_id_type=MESH,
        ).wait_recv()
    squares = parts[0, 0:16, :]
    for p in range(1, sides):
        squares = squares + parts[p, 0:16, :]
    scales[...] = lax.rsqrt(squares / (sides * 256) + norm_epsilon)
    scale_weights(groups, sides, parts, wts)
    gates_load.wait()
    mover.tick(-3)
    mover.tick(-2)

    def halo_copy():
        return pltpu.make_async_remote_copy(
            src_ref=halo_out, dst_ref=halo_in,
            send_sem=halo_sem.at[0], recv_sem=halo_sem.at[1],
            device_id={"seq": lax.rem(part + 1, peers)}, device_id_type=MESH,
        )

    def body(q, c):
        @pl.when(q < chunks)
        def _():
            for h in range(chunk // unit):
                mover.stage_5(q * (chunk // unit) + h)

        mover.tick(2 * q - 1)

        @pl.when(q < chunks)
        def _():
            first = lax.rem(q + chunks - 1, chunks) * (chunk // lanes)
            project(groups, q, first, rows_ref, wts, scales, pj)

        @pl.when(q == 0)
        def _():
            for n in range(3 * groups):
                pj_last[n] = pj[n]
                halo_out[:, lane_tile(n)] = pj[n, chunk - halo_rows :, :].astype(jnp.bfloat16)
            halo_copy().start()

        @pl.when(q == 1)
        def _():
            halo_copy().wait()
            seen = jnp.where(part > 0, 1.0, 0.0)
            for n in range(3 * groups):
                outs[n] = jnp.zeros((chunk, lanes), jnp.float32)
                outs[n, chunk - halo_rows :, :] = halo_in[:, lane_tile(n)].astype(jnp.float32) * seen
            short_part(groups, outs, tail, sfb, qs, pe)

        @pl.when(q == chunks)
        def _():
            pj[...] = pj_last[...]

        @pl.when(q > 0)
        def _():
            short_part(groups, pj, tail, sfb, qs, pe)

        mover.tick(2 * q)

        @pl.when(q > 0)
        def _():
            k = q - 1
            load_gates(k, gates, gs)
            medium_part(groups, pe, fb, qs, gs, ls)
            long_part(groups, modes, k, ls, lam, skb, pw, carry_ref, ys, inits)

        return c

    lax.fori_loop(0, chunks + 1, body, 0)

    for g in range(groups):
        for m in range(modes):
            states[0, g, m : m + 1, :] = carry_ref[g, m, 0:1, :]

    def state_copy(o):
        return pltpu.make_async_remote_copy(
            src_ref=states.at[0], dst_ref=states.at[o],
            send_sem=state_send.at[o], recv_sem=state_recv.at[o],
            device_id={"seq": lax.rem(part + o, peers)}, device_id_type=MESH,
        )

    for o in range(1, peers):
        state_copy(o).start()

    mover.sent()
    for o in range(1, sides):
        part_copy(o).wait_send()
    for o in range(1, peers):
        state_copy(o).wait()
    for g in range(groups):
        total = jnp.zeros((modes, lanes), jnp.float32)
        d = decay_ref[:, lane_tile(g)]
        for o in range(1, peers):
            weight = jnp.exp(d * (-1.0 * chunk * chunks * (o - 1)))
            total = total + jnp.where(part >= o, weight, 0.0) * states[o, g]
        for m in range(modes):
            incoming[g, m] = fill(total[m : m + 1])

    def finish(k, c):
        load_gates(k, gates, gs)
        finish_part(groups, modes, k, incoming, lam, pw, ys, inits, gs, outs)
        rows = pl.ds(pl.multiple_of(k * chunk, chunk), chunk)
        for g in range(groups):
            out_ref[rows, lane_tile(g)] = outs[g].astype(jnp.bfloat16)
        return c

    lax.fori_loop(0, chunks, finish, 0)


def in_vmem(n):
    return [pl.BlockSpec(memory_space=pltpu.VMEM)] * n


def vregs(*lead):
    return pltpu.VMEM(lead + (segs, lanes), jnp.float32)


def fused_call(resid, weight, gates, gain, short_filter, mr_filter, decays, residue, skip):
    length, width = resid.shape
    modes = decays.shape[0]
    groups, chunks = width // lanes, length // chunk
    sides, peers = lax.axis_size("chan"), lax.axis_size("seq")
    units = length // unit
    f32, bf16 = jnp.float32, jnp.bfloat16
    dma = pltpu.SemaphoreType.DMA
    anywhere = pl.BlockSpec(memory_space=pl.ANY)
    vmem = pl.BlockSpec(memory_space=pltpu.VMEM)
    return pl.pallas_call(
        functools.partial(fused_kernel, groups, modes, chunks, sides, peers),
        out_shape=jax.ShapeDtypeStruct((length, width), bf16),
        in_specs=[anywhere] * 3 + [vmem] * 6,
        out_specs=vmem,
        scratch_shapes=[
            pltpu.VMEM((chunks, chunk, sides * width), bf16),
            pltpu.VMEM((3, sides * width, width), bf16),
            pltpu.VMEM(gates.shape, bf16),
            pltpu.VMEM((length, width), bf16),
            pltpu.VMEM((sides, part_rows, lanes), f32),
            pltpu.VMEM((length // lanes, lanes), f32),
            pltpu.VMEM((3 * groups, chunk, lanes), f32),
            pltpu.VMEM((3 * groups, chunk, lanes), f32),
            pltpu.VMEM((halo_rows, 3 * width), bf16),
            pltpu.VMEM((halo_rows, 3 * width), bf16),
            pltpu.VMEM((peers, groups, modes, lanes), f32),
            pltpu.VMEM((3 * groups, chunk, lanes), f32),
            vregs(3 * groups, 2),
            vregs(9 * groups),
            vregs(groups, steps),
            vregs(groups, taps + steps),
            vregs(groups, taps),
            pltpu.VMEM((chunk * 2 * groups, lanes), f32),
            vregs(groups, steps),
            vregs(2, groups, modes),
            vregs(groups),
            vregs(5, groups, modes),
            vregs(groups, modes),
            vregs(groups, modes),
            vregs(chunks, groups, steps),
            vregs(chunks, groups, modes),
            dma((kinds,)),
            dma((units, waits)),
            dma((units,)),
            dma((sides,)),
            dma((sides,)),
            dma((peers,)),
            dma((peers,)),
            dma((2,)),
            dma,
            dma,
            dma,
        ],
        compiler_params=pltpu.CompilerParams(
            vmem_limit_bytes=60 << 20, collective_id=0, has_side_effects=True
        ),
    )(resid, weight, gates, gain, short_filter, mr_filter, decays, residue, skip)


def on_device(
    resid, norm_gain, feat_weight, short_filter, mr_filter, gates_lr, decay_rate, residue, skip_gain
):
    tokens, two, width = gates_lr.shape
    gates = gates_lr.reshape(tokens, two, width // lanes, lanes).transpose(0, 2, 1, 3)
    return fused_call(
        resid,
        jnp.transpose(feat_weight, (1, 0, 2)),
        gates.reshape(tokens * two * (width // lanes), lanes),
        norm_gain,
        short_filter,
        mr_filter,
        decay_rate,
        residue,
        skip_gain,
    )


def solution(mesh):
    in_specs = (
        P("seq", "chan"),
        P("chan"),
        P(None, None, "chan"),
        P(None, None, "chan"),
        P(None, "chan"),
        P("seq", None, "chan"),
        P(None, "chan"),
        P(None, "chan"),
        P("chan"),
    )
    return jax.shard_map(
        on_device, mesh=mesh, in_specs=in_specs, out_specs=P("seq", "chan"), check_vma=False
    )
```

time: 135 us -> 120 us (0.89)
  Pallas kernels: 126 us -> 118 us
  local copies, waits for them, and re-layouts: 5.48 us -> 2.26 us
  other arithmetic: 2.6 us -> 0 us
    pallas_call x1, Pallas kernels: 126 us -> 118 us  [fused_call(): pl.pallas_call(functools.partial(fused_kernel, groups, modes, chunks, sid...]
    unnamed x2 -> x1, local copies, waits for them, and re-layouts: 5.48 us -> 2.26 us
    mul x1 -> x0, other arithmetic: 1.36 us -> none  [on_device(): modal = residue * jnp.sqrt(-jnp.expm1(-2.0 * decay_rate))]
where the time goes in v3:
time: 120 us
  Pallas kernels  118 us (98%)
  local copies, waits for them, and re-layouts  2.26 us (2%)
    pallas_call x1, Pallas kernels, fused_call(): pl.pallas_call(functools.partial(fused_kernel, groups, modes, chunks, sid...  118 us

profile of v3, /device:TPU:0, one launch (start us, length us, event | category | flops | bytes accessed | tf_op | source)
XLA Modules:
  0.0 120.1 jit_solution(17883296389554972721)
XLA Ops:
  0.0 117.9 %shard_map.91 = bf16[2048,256]{1,0:T(8,128)(2,1)} custom-call(bf16[2048,256]{1,0:T(8,128)(2,1)} %resid_ref.1, bf16[3,4096,256]{2,1,0:T(8,128)(2,1)} %bitcast.6, bf16[8192,128]{1,0:T(8,128)(2,1)} %bitcast.7, bf16[256]{0:T(256)(128)(2,1)} %gain_ref.1, f32[3,3,256]{2,1,0:T(4,128)} %sf_ref.1, bf16[128,256]{1,0:T(8,128)(2,1)} %mr_ref.1, f32[16,256]{1,0:T(8,128)} %decay_ref.1, ...), custom_call_target="tpu_custom_call" | custom-call | tf_op jit(solution)/shard_map/pallas_call | solution.py:560
  117.9 2.3 %copy.12 = bf16[2048,256]{1,0:T(8,128)(2,1)} copy(bf16[2048,256]{1,0:T(8,128)(2,1)} %shard_map.91) | data formatting | bytes 2097152

commit v4 on v3

--- a/solution.py
+++ b/solution.py
@@ -14,8 +14,13 @@
 chunk = segs * steps
 taps = 128
 back = taps // steps
-block = 16
-group = 8
+phases = 4
+short_steps = steps // phases
+short_taps = taps // phases
+sums = ((0, 2), (1, 3), (0, 1), (2, 3), (4, 5))
+parts_of = phases + len(sums)
+halves = ((0, 2, 4), (1, 3, 5), (6, 7, 8))
+early = (1, 2, 3, 5, 7)
 
 
 def sublane():
@@ -46,8 +51,12 @@
 
         def taps_at(t, carry):
             rows = mr_ref[pl.ds(pl.multiple_of(t * 16, 16), 16), cols].astype(jnp.float32)
-            for i in range(16):
-                fb[g, t * 16 + i] = fill(rows[i : i + 1])
+            for j in range(16 // phases):
+                values = [fill(rows[phases * j + i : phases * j + i + 1]) for i in range(phases)]
+                for a, b in sums:
+                    values.append(values[a] + values[b])
+                for n, value in enumerate(values):
+                    fb[g, n, t * (16 // phases) + j] = value
             return carry
 
         lax.fori_loop(0, taps // 16, taps_at, 0)
@@ -68,7 +77,7 @@
     return ref[lead, pl.ds(r, segs, stride=steps), :]
 
 
-def short_part(groups, pj, tail, sfb, qs, pe):
+def short_part(groups, pj, tail, sfb, qs, ps):
     sub = sublane()
     for g in range(groups):
         names = [s * groups + g for s in range(3)]
@@ -86,49 +95,66 @@
             tail[n, 0] = turned[0]
             tail[n, 1] = turned[1]
 
-        def step(r, carry):
-            after, featured = [], []
-            for n, (one, two) in zip(names, carry):
-                now = strided(pj, n, r)
-                featured.append(sfb[n * 3] * now + sfb[n * 3 + 1] * one + sfb[n * 3 + 2] * two)
-                after.append((now, one))
-            product = (featured[1] * featured[2]).astype(jnp.bfloat16).astype(jnp.float32)
-            qs[g, r] = featured[0]
-            past = pe[g, taps + r]
-            for i in range(1, back + 1):
-                pe[g, taps - steps * i + r] = pltpu.roll(
-                    jnp.where(sub >= segs - i, past, product), i, 0
-                )
-            pe[g, taps + r] = product
-            return tuple(after)
-
-        lax.fori_loop(0, steps, step, tuple(old), unroll=4)
-
-
-def medium_part(groups, pe, fb, qs, gs, ls):
+        def step(n, carry):
+            products = []
+            for i in range(phases):
+                r = n * phases + i
+                after, featured = [], []
+                for name, (one, two) in zip(names, carry):
+                    now = strided(pj, name, r)
+                    featured.append(
+                        sfb[name * 3] * now + sfb[name * 3 + 1] * one + sfb[name * 3 + 2] * two
+                    )
+                    after.append((now, one))
+                carry = tuple(after)
+                products.append((featured[1] * featured[2]).astype(jnp.bfloat16).astype(jnp.float32))
+                qs[g, r] = featured[0]
+            past = [ps[g, i, short_taps + n] for i in range(phases)]
+            for shift in range(back + 1):
+                values = products
+                if shift > 0:
+                    values = [
+                        pltpu.roll(jnp.where(sub >= segs - shift, old, new), shift, 0)
+                        for old, new in zip(past, products)
+                    ]
+                values = list(values)
+                for x, y in sums:
+                    values.append(values[x] + values[y])
+                for i, value in enumerate(values):
+                    ps[g, i, short_taps - shift * short_steps + n] = value
+            return carry
+
+        lax.fori_loop(0, short_steps, step, tuple(old))
+
+
+def medium_part(groups, ps, fb, qs, gs, ls, yb):
     for g in range(groups):
-
-        def at_block(b, carry):
-            def taps_at(t, sums):
-                base = taps + b * block - t * group
-                window = [pe[g, base - group + 1 + i] for i in range(block + group - 1)]
-                sums = list(sums)
-                for j in range(group):
-                    tap = fb[g, t * group + j]
-                    for i in range(block):
-                        sums[i] = sums[i] + tap * window[group - 1 + i - j]
-                return tuple(sums)
-
-            zero = jnp.zeros((segs, lanes), jnp.float32)
-            sums = lax.fori_loop(0, taps // group, taps_at, (zero,) * block)
-            for i in range(block):
-                r = b * block + i
-                mixed = (qs[g, r] * sums[i]).astype(jnp.bfloat16).astype(jnp.float32)
+        for n in range(parts_of):
+            begin = -1 if n in early else 0
+            totals = {}
+            for j in range(short_taps):
+                tap = fb[g, n, j]
+                for i in range(begin, short_steps):
+                    term = tap * ps[g, n, short_taps + i - j]
+                    totals[i] = term if j == 0 else totals[i] + term
+            for i in range(begin, short_steps):
+                yb[n, i + 1] = totals[i]
+
+        def half(which, i):
+            even, odd, both = halves[which]
+            n = i // 2
+            if i % 2 == 0:
+                return yb[even, n + 1] + yb[odd, n]
+            return yb[both, n + 1] - yb[even, n + 1] - yb[odd, n + 1]
+
+        before = half(1, -1)
+        for m in range(steps // 2):
+            evens, odds, both = half(0, m), half(1, m), half(2, m)
+            for r, medium in ((2 * m, evens + before), (2 * m + 1, both - evens - odds)):
+                mixed = (qs[g, r] * medium).astype(jnp.bfloat16).astype(jnp.float32)
                 gate = gate_at(gs, groups, g, 1, r)
                 ls[g, r] = (gate * mixed).astype(jnp.bfloat16).astype(jnp.float32)
-            return carry
-
-        lax.fori_loop(0, steps // block, at_block, 0)
+            before = odds
 
 
 def long_part(groups, modes, k, ls, lam, skb, pw, carry_ref, ys, inits):
@@ -176,7 +202,7 @@
                 state = lam[0, g, m] * states[m]
                 total = total + state
                 after.append(state)
-            outs[g, pl.ds(r, segs, stride=steps), :] = gate_at(gs, groups, g, 0, r) * total
+            outs[g, pl.ds(pl.multiple_of(r * segs, segs), segs), :] = gate_at(gs, groups, g, 0, r) * total
             return tuple(after)
 
         lax.fori_loop(0, steps, step, tuple(starts), unroll=2)
@@ -194,7 +220,6 @@
 MESH = pl.DeviceIdType.MESH
 kinds = 10
 waits = 8
-halo_rows = taps + 16
 unit = 128
 part_rows = 24
 
@@ -373,8 +398,8 @@
     groups, modes, chunks, sides, peers,
     resid_ref, weight_hbm, gates_hbm, gain_ref, sf_ref, mr_ref, decay_ref, residue_ref, skip_ref,
     out_ref,
-    rows_ref, wts, gates, own_rows, parts, scales, pj, pj_last, halo_out, halo_in, states, outs,
-    tail, sfb, qs, pe, fb, gs, ls, lam, skb, pw, carry_ref, incoming, ys, inits,
+    rows_ref, wts, gates, own_rows, parts, scales, pj, pj_last, halo_in, tail_in, states, outs,
+    tail, sfb, qs, ps, yb, fb, gs, ls, lam, skb, pw, carry_ref, incoming, ys, inits,
     send_sem, recv_sem, own_sem, gain_send, gain_recv, state_send, state_recv, halo_sem, weight_sem, own_load_sem, gates_sem,
 ):
     me, part = lax.axis_index("chan"), lax.axis_index("seq")
@@ -424,7 +449,7 @@
     mover.tick(-5)
     carry_ref[...] = jnp.zeros_like(carry_ref)
     tail[...] = jnp.zeros_like(tail)
-    pe[...] = jnp.zeros_like(pe)
+    ps[...] = jnp.zeros_like(ps)
     load.wait()
     mover.tick(-4)
     for o in range(1, sides):
@@ -443,12 +468,19 @@
     mover.tick(-3)
     mover.tick(-2)
 
-    def halo_copy():
-        return pltpu.make_async_remote_copy(
-            src_ref=halo_out, dst_ref=halo_in,
-            send_sem=halo_sem.at[0], recv_sem=halo_sem.at[1],
-            device_id={"seq": lax.rem(part + 1, peers)}, device_id_type=MESH,
+    def halo_copies():
+        sent = (
+            (ps.at[:, pl.ds(0, phases), pl.ds(short_taps, short_steps), pl.ds(segs - back, back), :], halo_in),
+            (tail.at[:, :, pl.ds(0, 1), :], tail_in),
         )
+        return [
+            pltpu.make_async_remote_copy(
+                src_ref=source, dst_ref=target,
+                send_sem=halo_sem.at[2 * n], recv_sem=halo_sem.at[2 * n + 1],
+                device_id={"seq": lax.rem(part + 1, peers)}, device_id_type=MESH,
+            )
+            for n, (source, target) in enumerate(sent)
+        ]
 
     def body(q, c):
         @pl.when(q < chunks)
@@ -465,19 +497,23 @@
 
         @pl.when(q == 0)
         def _():
-            for n in range(3 * groups):
-                pj_last[n] = pj[n]
-                halo_out[:, lane_tile(n)] = pj[n, chunk - halo_rows :, :].astype(jnp.bfloat16)
-            halo_copy().start()
+            pj_last[...] = pj[...]
+            short_part(groups, pj, tail, sfb, qs, ps)
+            for copy in halo_copies():
+                copy.start()
 
         @pl.when(q == 1)
         def _():
-            halo_copy().wait()
+            for copy in halo_copies():
+                copy.wait()
             seen = jnp.where(part > 0, 1.0, 0.0)
+            for g in range(groups):
+                for i in range(phases):
+                    for n in range(short_steps):
+                        ps[g, i, short_taps + n, segs - back :, :] = halo_in[g, i, n] * seen
             for n in range(3 * groups):
-                outs[n] = jnp.zeros((chunk, lanes), jnp.float32)
-                outs[n, chunk - halo_rows :, :] = halo_in[:, lane_tile(n)].astype(jnp.float32) * seen
-            short_part(groups, outs, tail, sfb, qs, pe)
+                for i in range(2):
+                    tail[n, i, 0:1, :] = tail_in[n, i] * seen
 
         @pl.when(q == chunks)
         def _():
@@ -485,7 +521,7 @@
 
         @pl.when(q > 0)
         def _():
-            short_part(groups, pj, tail, sfb, qs, pe)
+            short_part(groups, pj, tail, sfb, qs, ps)
 
         mover.tick(2 * q)
 
@@ -493,7 +529,7 @@
         def _():
             k = q - 1
             load_gates(k, gates, gs)
-            medium_part(groups, pe, fb, qs, gs, ls)
+            medium_part(groups, ps, fb, qs, gs, ls, yb)
             long_part(groups, modes, k, ls, lam, skb, pw, carry_ref, ys, inits)
 
         return c
@@ -531,9 +567,14 @@
     def finish(k, c):
         load_gates(k, gates, gs)
         finish_part(groups, modes, k, incoming, lam, pw, ys, inits, gs, outs)
-        rows = pl.ds(pl.multiple_of(k * chunk, chunk), chunk)
         for g in range(groups):
-            out_ref[rows, lane_tile(g)] = outs[g].astype(jnp.bfloat16)
+            for seg in range(segs):
+                for r in range(0, steps, 16):
+                    pieces = [
+                        outs[g, pl.ds((r + half) * segs + seg, 8, stride=segs), :] for half in (0, 8)
+                    ]
+                    rows = pl.ds(pl.multiple_of(k * chunk + seg * steps + r, 16), 16)
+                    out_ref[rows, lane_tile(g)] = jnp.concatenate(pieces, axis=0).astype(jnp.bfloat16)
         return c
 
     lax.fori_loop(0, chunks, finish, 0)
@@ -571,15 +612,16 @@
             pltpu.VMEM((length // lanes, lanes), f32),
             pltpu.VMEM((3 * groups, chunk, lanes), f32),
             pltpu.VMEM((3 * groups, chunk, lanes), f32),
-            pltpu.VMEM((halo_rows, 3 * width), bf16),
-            pltpu.VMEM((halo_rows, 3 * width), bf16),
+            pltpu.VMEM((groups, phases, short_steps, back, lanes), f32),
+            pltpu.VMEM((3 * groups, 2, 1, lanes), f32),
             pltpu.VMEM((peers, groups, modes, lanes), f32),
-            pltpu.VMEM((3 * groups, chunk, lanes), f32),
+            pltpu.VMEM((groups, chunk, lanes), f32),
             vregs(3 * groups, 2),
             vregs(9 * groups),
             vregs(groups, steps),
-            vregs(groups, taps + steps),
-            vregs(groups, taps),
+            vregs(groups, parts_of, short_taps + short_steps),
+            vregs(parts_of, short_steps + 1),
+            vregs(groups, parts_of, short_taps),
             pltpu.VMEM((chunk * 2 * groups, lanes), f32),
             vregs(groups, steps),
             vregs(2, groups, modes),
@@ -596,7 +638,7 @@
             dma((sides,)),
             dma((peers,)),
             dma((peers,)),
-            dma((2,)),
+            dma((4,)),
             dma,
             dma,
             dma,

time: 120 us -> 106 us (0.88)
  Pallas kernels: 118 us -> 104 us
    pallas_call x1, Pallas kernels: 118 us -> 104 us  [fused_call(): pl.pallas_call(functools.partial(fused_kernel, groups, modes, chunks, sid...]
where the time goes in v4:
time: 106 us
  Pallas kernels  104 us (98%)
  local copies, waits for them, and re-layouts  2.26 us (2%)
    pallas_call x1, Pallas kernels, fused_call(): pl.pallas_call(functools.partial(fused_kernel, groups, modes, chunks, sid...  104 us
    unnamed x1, local copies, waits for them, and re-layouts  2.26 us

profile of v4, /device:TPU:0, one launch (start us, length us, event | category | flops | bytes accessed | tf_op | source)
XLA Modules:
  0.0 106.3 jit_solution(2410576084001263913)
XLA Ops:
  0.0 104.0 %shard_map.91 = bf16[2048,256]{1,0:T(8,128)(2,1)} custom-call(bf16[2048,256]{1,0:T(8,128)(2,1)} %resid_ref.1, bf16[3,4096,256]{2,1,0:T(8,128)(2,1)} %bitcast.6, bf16[8192,128]{1,0:T(8,128)(2,1)} %bitcast.7, bf16[256]{0:T(256)(128)(2,1)} %gain_ref.1, f32[3,3,256]{2,1,0:T(4,128)} %sf_ref.1, bf16[128,256]{1,0:T(8,128)(2,1)} %mr_ref.1, f32[16,256]{1,0:T(8,128)} %decay_ref.1, ...), custom_call_target="tpu_custom_call" | custom-call | tf_op jit(solution)/shard_map/pallas_call | solution.py:601
  104.0 2.3 %copy.12 = bf16[2048,256]{1,0:T(8,128)(2,1)} copy(bf16[2048,256]{1,0:T(8,128)(2,1)} %shard_map.91) | data formatting | bytes 2097152

commit v5 on v4

--- a/solution.py
+++ b/solution.py
@@ -325,12 +325,12 @@
         self.own(q).start()
 
     def stage_2(self, q):
-        self.arrived(q, 2)
-        self.start(q, 5, 6)
         self.arrived(q, 0)
         self.start(q, 3)
         self.arrived(q, 1)
         self.start(q, 4)
+        self.arrived(q, 2)
+        self.start(q, 5, 6)
 
     def stage_3(self, q):
         self.own(q).wait()
@@ -345,7 +345,7 @@
         self.arrived(q, 7)
 
     def tick(self, t):
-        stages = ((4, self.stage_3), (6, self.stage_2), (8, self.stage_1), (3, self.stage_4))
+        stages = ((5, self.stage_3), (8, self.stage_2), (11, self.stage_1), (3, self.stage_4))
         for lead, stage in stages:
             if isinstance(t, int):
                 if 0 <= t + lead < self.units:
@@ -354,7 +354,7 @@
                 pl.when(t + lead < self.units)(functools.partial(stage, t + lead))
 
 
-def scale_weights(groups, peers, parts, wts):
+def scale_weights(groups, begin, end, parts, wts):
     def body(j, c):
         for h in range(2):
             row = parts[j, 16 + h : 17 + h, :]
@@ -366,7 +366,7 @@
                     wts[s, rows, lane_tile(g)] = (value * column).astype(jnp.bfloat16)
         return c
 
-    lax.fori_loop(0, peers, body, 0)
+    lax.fori_loop(begin, end, body, 0)
 
 
 def square_rows(tokens, own_rows, parts, me):
@@ -421,21 +421,19 @@
         pl.semaphore_signal(barrier, inc=1, device_id={"chan": lax.rem(me + o, sides)}, device_id_type=MESH)
     for o in range(1, peers):
         pl.semaphore_signal(barrier, inc=1, device_id={"seq": lax.rem(part + o, peers)}, device_id_type=MESH)
-    pl.semaphore_wait(barrier, sides + peers - 2)
-
     units = chunks * chunk // unit
     mover = Mover(units, resid_ref, own_rows, rows_ref, send_sem, recv_sem, own_sem)
-    mover.tick(-8)
-    mover.tick(-7)
+    pl.semaphore_wait(barrier, sides + peers - 2)
+    mover.tick(-11)
+    mover.tick(-10)
+    mover.tick(-9)
 
     gain = gain_ref[...].reshape(1, 256).astype(jnp.float32)
     parts[mover.here, 16:17, :] = gain[:, lane_tile(0)]
     parts[mover.here, 17:18, :] = gain[:, lane_tile(1)]
     own_load.wait()
     square_rows(chunks * chunk, own_rows, parts, mover.here)
-    mover.tick(-6)
-    skip = skip_ref[...].reshape(1, 256)
-    set_constants(groups, modes, sf_ref, mr_ref, decay_ref, residue_ref, skip, sfb, fb, lam, skb, pw)
+    mover.tick(-8)
 
     def part_copy(o):
         return pltpu.make_async_remote_copy(
@@ -446,12 +444,16 @@
 
     for o in range(1, sides):
         part_copy(o).start()
-    mover.tick(-5)
+    mover.tick(-7)
+    skip = skip_ref[...].reshape(1, 256)
+    set_constants(groups, modes, sf_ref, mr_ref, decay_ref, residue_ref, skip, sfb, fb, lam, skb, pw)
+    mover.tick(-6)
     carry_ref[...] = jnp.zeros_like(carry_ref)
     tail[...] = jnp.zeros_like(tail)
     ps[...] = jnp.zeros_like(ps)
     load.wait()
-    mover.tick(-4)
+    gates_load.wait()
+    mover.tick(-5)
     for o in range(1, sides):
         source = lax.rem(me + sides - o, sides)
         pltpu.make_async_remote_copy(
@@ -463,8 +465,8 @@
     for p in range(1, sides):
         squares = squares + parts[p, 0:16, :]
     scales[...] = lax.rsqrt(squares / (sides * 256) + norm_epsilon)
-    scale_weights(groups, sides, parts, wts)
-    gates_load.wait()
+    mover.tick(-4)
+    scale_weights(groups, 0, sides, parts, wts)
     mover.tick(-3)
     mover.tick(-2)
 

time: 106 us -> 105 us (level)
  Pallas kernels: 104 us -> 102 us
    pallas_call x1, Pallas kernels: 104 us -> 102 us  [fused_call(): pl.pallas_call(functools.partial(fused_kernel, groups, modes, chunks, sid...]
where the time goes in v5:
time: 105 us
  Pallas kernels  102 us (97%)
  local copies, waits for them, and re-layouts  2.26 us (2%)
    pallas_call x1, Pallas kernels, fused_call(): pl.pallas_call(functools.partial(fused_kernel, groups, modes, chunks, sid...  102 us
    unnamed x1, local copies, waits for them, and re-layouts  2.26 us

profile of v5, /device:TPU:0, one launch (start us, length us, event | category | flops | bytes accessed | tf_op | source)
XLA Modules:
  0.0 104.7 jit_solution(8164945755118776681)
XLA Ops:
  0.0 102.5 %shard_map.91 = bf16[2048,256]{1,0:T(8,128)(2,1)} custom-call(bf16[2048,256]{1,0:T(8,128)(2,1)} %resid_ref.1, bf16[3,4096,256]{2,1,0:T(8,128)(2,1)} %bitcast.6, bf16[8192,128]{1,0:T(8,128)(2,1)} %bitcast.7, bf16[256]{0:T(256)(128)(2,1)} %gain_ref.1, f32[3,3,256]{2,1,0:T(4,128)} %sf_ref.1, bf16[128,256]{1,0:T(8,128)(2,1)} %mr_ref.1, f32[16,256]{1,0:T(8,128)} %decay_ref.1, ...), custom_call_target="tpu_custom_call" | custom-call | tf_op jit(solution)/shard_map/pallas_call | solution.py:603
  102.5 2.3 %copy.12 = bf16[2048,256]{1,0:T(8,128)(2,1)} copy(bf16[2048,256]{1,0:T(8,128)(2,1)} %shard_map.91) | data formatting | bytes 2097152

commit v6 on v5

--- a/solution.py
+++ b/solution.py
@@ -173,7 +173,7 @@
             return tuple(after)
 
         zero = jnp.zeros((segs, lanes), jnp.float32)
-        ends = lax.fori_loop(0, steps, step, (zero,) * modes, unroll=2)
+        ends = lax.fori_loop(0, steps, step, (zero,) * modes, unroll=4)
         for m in range(modes):
             scan = ends[m]
             for n in range(3):
@@ -205,7 +205,7 @@
             outs[g, pl.ds(pl.multiple_of(r * segs, segs), segs), :] = gate_at(gs, groups, g, 0, r) * total
             return tuple(after)
 
-        lax.fori_loop(0, steps, step, tuple(starts), unroll=2)
+        lax.fori_loop(0, steps, step, tuple(starts), unroll=4)
 
 
 def load_gates(k, gates, gs):

time: 105 us -> 102 us (0.971)
  Pallas kernels: 102 us -> 99.8 us
    pallas_call x1, Pallas kernels: 102 us -> 99.8 us  [fused_call(): pl.pallas_call(functools.partial(fused_kernel, groups, modes, chunks, sid...]
where the time goes in v6:
time: 102 us
  Pallas kernels  99.8 us (98%)
  local copies, waits for them, and re-layouts  2.26 us (2%)
    pallas_call x1, Pallas kernels, fused_call(): pl.pallas_call(functools.partial(fused_kernel, groups, modes, chunks, sid...  99.8 us
    unnamed x1, local copies, waits for them, and re-layouts  2.26 us

profile of v6, /device:TPU:0, one launch (start us, length us, event | category | flops | bytes accessed | tf_op | source)
XLA Modules:
  0.0 102.0 jit_solution(4086653528854835808)
XLA Ops:
  0.0 99.8 %shard_map.91 = bf16[2048,256]{1,0:T(8,128)(2,1)} custom-call(bf16[2048,256]{1,0:T(8,128)(2,1)} %resid_ref.1, bf16[3,4096,256]{2,1,0:T(8,128)(2,1)} %bitcast.6, bf16[8192,128]{1,0:T(8,128)(2,1)} %bitcast.7, bf16[256]{0:T(256)(128)(2,1)} %gain_ref.1, f32[3,3,256]{2,1,0:T(4,128)} %sf_ref.1, bf16[128,256]{1,0:T(8,128)(2,1)} %mr_ref.1, f32[16,256]{1,0:T(8,128)} %decay_ref.1, ...), custom_call_target="tpu_custom_call" | custom-call | tf_op jit(solution)/shard_map/pallas_call | solution.py:603
  99.8 2.3 %copy.12 = bf16[2048,256]{1,0:T(8,128)(2,1)} copy(bf16[2048,256]{1,0:T(8,128)(2,1)} %shard_map.91) | data formatting | bytes 2097152
